TPU v7x, 256 devices: a whole 4x4x8 slice. The times are simulated.
256 devices in a mesh: role: 4 (over y), seq: 16 (over x_lo, z), mp: 4 (over x_hi, core).
Axes of the slice: x: 4 (x_hi: 2, x_lo: 2; x = x_hi * 2 + x_lo), y: 4, z: 8, core: 2. Of those that a mesh axis runs over, the one named last changes fastest.
Arguments:
- gen_heads: bfloat16 [1024, 4096], P(None, 'seq'), may hold values from -6 to 6
- gen_resid: bfloat16 [1024, 5120], P('seq', 'mp'), may hold values from -6 to 6
- gen_out_w: bfloat16 [4096, 5120], P('seq', 'mp'), may hold values from -0.09375 to 0.09375
- gen_time_w: bfloat16 [256, 5120], P(None, 'mp'), may hold values from -0.375 to 0.375
- noise: bfloat16 [1024, 5120], P('seq', 'mp'), may hold values from -6 to 6
- steps: int32 [3], replicated, may hold values from 20 to 979
- teacher_qkv: bfloat16 [5120, 3, 4096], P('mp', None, 'seq'), may hold values from -0.078125 to 0.078125
- teacher_out: bfloat16 [4096, 5120], P('seq', 'mp'), may hold values from -0.09375 to 0.09375
- teacher_time: bfloat16 [256, 3, 5120], P(None, None, 'mp'), may hold values from -0.375 to 0.375
- teacher_norm: float32 [2, 4096], P(None, 'seq'), may hold values from 0.5 to 1.5
- critic_qkv: bfloat16 [5120, 3, 4096], P('mp', None, 'seq'), may hold values from -0.078125 to 0.078125
- critic_out: bfloat16 [4096, 5120], P('seq', 'mp'), may hold values from -0.09375 to 0.09375
- critic_time: bfloat16 [256, 3, 5120], P(None, None, 'mp'), may hold values from -0.375 to 0.375
- critic_norm: float32 [2, 4096], P(None, 'seq'), may hold values from 0.5 to 1.5
Outputs:
- latent: bfloat16 [1024, 5120], P('seq', 'mp')
- weight_grad: bfloat16 [4096, 5120], P('seq', 'mp')
All inputs are finite; a program needn't handle non-finite values.
Results may differ from a plain program's by a relative error of at most 0.012.
Values may be sent and summed in bfloat16 or wider, within the bound.
A program may use at most 64 MiB of HBM per device.

v0:
```python
import math

import jax
import jax.numpy as jnp
from jax import lax
from jax.sharding import PartitionSpec as P

D = 5120
HEAD_DIM = 128


def time_embed(step_value, width):
    half_width = width // 2
    positions = jnp.arange(half_width, dtype=jnp.float32)
    frequencies = jnp.exp(positions * (-math.log(10000.0) / half_width))
    angles = step_value.astype(jnp.float32) * frequencies
    return jnp.concatenate([jnp.cos(angles), jnp.sin(angles)]).astype(jnp.bfloat16)


def head_norm(values, gains):
    factor = lax.rsqrt(jnp.mean(values * values, axis=-1, keepdims=True) + 1e-06)
    return (values * factor * gains).astype(jnp.bfloat16)


def attend(query_norm, key_norm, value_rows):
    full_length, heads_here, head_width = query_norm.shape
    query_blocks = query_norm.reshape(
        full_length // full_length, full_length, heads_here, head_width
    )

    def one_block(query_block):
        logits = jnp.einsum(
            "qhd,khd->hqk", query_block, key_norm, preferred_element_type=jnp.float32
        ) * (1.0 / math.sqrt(head_width))
        expanded = jnp.exp(logits)
        probs = (expanded / jnp.sum(expanded, axis=2, keepdims=True)).astype(jnp.bfloat16)
        return jnp.einsum(
            "hqk,khd->qhd", probs, value_rows, preferred_element_type=jnp.float32
        ).astype(jnp.bfloat16)

    head_out = lax.map(one_block, query_blocks)
    return head_out.reshape(full_length, heads_here * head_width)


def on_device(
    gen_heads,
    gen_resid,
    gen_out_w,
    gen_time_w,
    noise,
    steps,
    teacher_qkv,
    teacher_out,
    teacher_time,
    teacher_norm,
    critic_qkv,
    critic_out,
    critic_time,
    critic_norm,
):
    full_length = gen_heads.shape[0]
    head_cols = gen_heads.shape[1]
    embed_width = gen_time_w.shape[0]
    gen_gate = jnp.dot(
        time_embed(steps[0], embed_width)[None, :], gen_time_w, preferred_element_type=jnp.float32
    )[0]
    block = gen_heads
    gen_proj = lax.psum_scatter(
        jnp.dot(block, gen_out_w, preferred_element_type=jnp.float32),
        "seq",
        scatter_dimension=0,
        tiled=True,
    )
    latent = (gen_resid.astype(jnp.float32) + gen_gate * gen_proj).astype(jnp.bfloat16)
    role_index = lax.axis_index("role")
    level = steps[1 + role_index // 2]
    use_critic = role_index % 2 == 1
    w_qkv = jnp.where(use_critic, critic_qkv, teacher_qkv)
    w_out = jnp.where(use_critic, critic_out, teacher_out)
    w_time = jnp.where(use_critic, critic_time, teacher_time)
    w_norm = jnp.where(use_critic, critic_norm, teacher_norm)
    noise_level = level.astype(jnp.float32) / 1000.0
    noisy = (
        (1.0 - noise_level) * latent.astype(jnp.float32) + noise_level * noise.astype(jnp.float32)
    ).astype(jnp.bfloat16)
    modulation = jnp.einsum(
        "f,fkd->kd", time_embed(level, embed_width), w_time, preferred_element_type=jnp.float32
    )
    shift_vec = modulation[0]
    scale_vec = modulation[1]
    gate_vec = modulation[2]
    gathered = lax.all_gather(noisy, "seq", axis=0, tiled=True)
    partial_squares = jnp.sum(jnp.square(gathered.astype(jnp.float32)), axis=1)
    scaled = (gathered.astype(jnp.float32) * (1.0 + scale_vec)).astype(jnp.bfloat16)
    flat_w = w_qkv.reshape(w_qkv.shape[0], 3 * head_cols)
    projected = jnp.dot(scaled, flat_w, preferred_element_type=jnp.float32)
    shift_proj = jnp.dot(
        shift_vec.astype(jnp.bfloat16)[None, :], flat_w, preferred_element_type=jnp.float32
    )[0]
    projected, squares, shift_proj = lax.psum((projected, partial_squares, shift_proj), "mp")
    mixed = projected * lax.rsqrt(squares / D + 1e-06)[:, None] + shift_proj
    heads_here = head_cols // HEAD_DIM
    mixed = mixed.reshape(full_length, 3, heads_here, HEAD_DIM)
    gains = w_norm.reshape(2, heads_here, HEAD_DIM)
    query_norm = head_norm(mixed[:, 0], gains[0])
    key_norm = head_norm(mixed[:, 1], gains[1])
    value_rows = mixed[:, 2].astype(jnp.bfloat16)
    head_out = attend(query_norm, key_norm, value_rows)
    weight_sign = jnp.where(use_critic, 0.5, -0.5)
    block = head_out
    summed_rows = lax.psum_scatter(
        weight_sign * (gate_vec * jnp.dot(block, w_out, preferred_element_type=jnp.float32)),
        ("role", "seq"),
        scatter_dimension=0,
        tiled=True,
    )
    grad_rows = lax.all_gather(
        (gen_gate * summed_rows).astype(jnp.bfloat16), ("role", "seq"), axis=0, tiled=True
    )
    weight_grad = lax.dot_general(
        gen_heads, grad_rows, (((0,), (0,)), ((), ())), preferred_element_type=jnp.float32
    )
    return (latent, weight_grad.astype(jnp.bfloat16))


def solution(mesh):
    in_specs = (
        P(None, "seq"),
        P("seq", "mp"),
        P("seq", "mp"),
        P(None, "mp"),
        P("seq", "mp"),
        P(),
        P("mp", None, "seq"),
        P("seq", "mp"),
        P(None, None, "mp"),
        P(None, "seq"),
        P("mp", None, "seq"),
        P("seq", "mp"),
        P(None, None, "mp"),
        P(None, "seq"),
    )
    out_specs = (P("seq", "mp"), P("seq", "mp"))
    return jax.shard_map(
        on_device, mesh=mesh, in_specs=in_specs, out_specs=out_specs, check_vma=False
    )
```

profile of v0, /device:TPU:2, one launch (start us, length us, event | category | flops | bytes accessed | tf_op | source)
XLA Modules:
  0.0 897.4 jit_solution(10704743921336881278)
XLA Ops:
  7.2 1.0 copy-done
  8.3 4.2 fusion.30
  12.6 0.6 copy-done.11
  13.1 0.6 fusion.29
  15.1 0.2 convolution_reduce_fusion
  15.3 83.3 %reduce-scatter.3.cloned.1.call-done = f32[64,1280]{1,0:T(8,128)} async-done(((f32[1024,1280]{1,0:T(8,128)}), f32[64,1280]{1,0:T(8,128)}) %reduce-scatter.3.cloned.1.call-update) | async-done | bytes 327696 | tf_op jit(solution)/shard_map/reduce_scatter | solution.py:68
  98.6 1.8 add_convert_fusion
  100.6 2.1 fusion.8
  102.7 4.1 copy.22
  106.9 2.3 copy.21
  109.2 1.8 broadcast_select_fusion
  111.0 58.8 %all-gather.3.cloned.1.call-done = bf16[1024,1280]{1,0:T(8,128)(2,1)} async-done(((bf16[64,1280]{1,0:T(8,128)(2,1)}), bf16[1024,1280]{1,0:T(8,128)(2,1)}) %all-gather.3.cloned.1.call-update) | async-done | bytes 2621456 | tf_op jit(solution)/shard_map/all_gather | solution.py:92
  169.7 5.7 fusion.4
  175.5 0.6 convolution_reduce_fusion.1
  176.2 2.3 fusion.2
  178.5 7.3 all-reduce
  185.8 67.8 %all-reduce.3.cloned.1.call-done = f32[1024,768]{1,0:T(8,128)} async-done(((f32[1024,768]{1,0:T(8,128)}), f32[1024,768]{1,0:T(8,128)}) %all-reduce.3.cloned.1.call-update) | async-done | bytes 3145744 | tf_op jit(solution)/shard_map/psum | solution.py:100
  253.6 3.9 multiply_add_fusion
  257.5 5.2 reshape.60
  262.8 1.6 slice.43
  264.3 1.7 fusion.27
  266.0 1.1 copy.32
  267.1 0.4 multiply_reduce_fusion
  267.5 0.4 multiply_reduce_fusion.1
  267.9 1.9 fusion
  269.9 1.6 fusion.11
  271.5 3.2 multiply_multiply_fusion
  274.8 312.9 %reduce-scatter.5.cloned.1.call-done = f32[16,1280]{1,0:T(8,128)} async-done(((f32[1024,1280]{1,0:T(8,128)}), f32[16,1280]{1,0:T(8,128)}) %reduce-scatter.5.cloned.1.call-update) | async-done | bytes 81936 | tf_op jit(solution)/shard_map/reduce_scatter | solution.py:111
  587.7 1.5 multiply_convert_fusion.4
  589.2 298.0 %all-gather.5.cloned.1.call-done = bf16[1024,1280]{1,0:T(8,128)(2,1)} async-done(((bf16[16,1280]{1,0:T(8,128)(2,1)}), bf16[1024,1280]{1,0:T(8,128)(2,1)}) %all-gather.5.cloned.1.call-update) | async-done | bytes 2621456 | tf_op jit(solution)/shard_map/all_gather | solution.py:117
  887.2 2.6 fusion.7
  889.8 1.1 copy.27
  (45 shorter events, 0.6 us)
Async XLA Ops:
  7.2 1.1 copy-start
  7.2 91.4 %reduce-scatter.3.cloned.1.call-start = ((), (), s32[]{:S(2)}) async-start(), calls=%async_computation.2 | async-start | bytes 5570560 | tf_op jit(solution)/shard_map/reduce_scatter | solution.py:68
  12.4 0.7 copy-start.11
  12.5 2.6 copy-start.6
  12.5 86.2 %copy-start.8 = (bf16[64,1280]{1,0:T(8,128)(2,1)S(1)}, bf16[64,1280]{1,0:T(8,128)(2,1)}, u32[]{:S(2)}) copy-start(bf16[64,1280]{1,0:T(8,128)(2,1)} %param.18) | copy-start | bytes 491524
  12.5 88.2 %copy-start.1 = (bf16[256,3,1280]{2,0,1:T(8,128)(2,1)S(1)}, bf16[256,3,1280]{2,0,1:T(8,128)(2,1)}, u32[]{:S(2)}) copy-start(bf16[256,3,1280]{2,0,1:T(8,128)(2,1)} %param.26) | copy-start | bytes 5898244
  12.5 157.2 %all-gather.3.cloned.1.call-start = ((), (), s32[]{:S(2)}) async-start(), calls=%async_computation.3 | async-start | bytes 2785280 | tf_op jit(solution)/shard_map/all_gather | solution.py:92
  100.5 153.2 %all-reduce.3.cloned.1.call-start = ((), (), s32[]{:S(2)}) async-start(), calls=%async_computation.4 | async-start | bytes 6291456 | tf_op jit(solution)/shard_map/psum | solution.py:100
  102.7 4.1 copy-start.2
  175.4 0.7 copy-start.9
  175.4 0.8 copy-start.10
  175.4 412.3 %reduce-scatter.5.cloned.1.call-start = ((), (), s32[]{:S(2)}) async-start(), calls=%async_computation.5 | async-start | bytes 5324800 | tf_op jit(solution)/shard_map/reduce_scatter | solution.py:111
  267.9 1.9 copy-start.7
  269.8 1.7 copy-start.4
  269.8 1.6 copy-start.5
  274.7 612.5 %copy-start.3 = (bf16[1024,256]{1,0:T(8,128)(2,1)S(1)}, bf16[1024,256]{1,0:T(8,128)(2,1)}, u32[]{:S(2)}) copy-start(bf16[1024,256]{1,0:T(8,128)(2,1)} %param.14) | copy-start | bytes 1572868
  274.7 612.4 %all-gather.5.cloned.1.call-start = ((), (), s32[]{:S(2)}) async-start(), calls=%async_computation.6 | async-start | bytes 2662400 | tf_op jit(solution)/shard_map/all_gather | solution.py:117
Sparse Core Ops, SparseCore 0:
  12.6 85.9 reduce-scatter.2
  101.0 68.6 all-gather.2
  175.6 78.0 all-reduce.2
  274.9 312.7 reduce-scatter.4
  589.9 297.2 all-gather.4
where the time goes:
time: 910 us; the launch traced here: 897 us
  waiting for transfers between devices  821 us (90%)
  matrix products  22.2 us (2%)
  local copies, waits for them, and re-layouts  19.3 us (2%)
  between operations  15.4 us (2%)
  other arithmetic  12.2 us (1%)
    reduce_scatter x1, waiting for transfers between devices, on_device(): lax.psum_scatter(weight_sign * (gate_vec * jnp.dot(block, w_out, preferre...  313 us
    all_gather x1, waiting for transfers between devices, on_device(): lax.all_gather((gen_gate * summed_rows).astype(jnp.bfloat16), ('role', 's...  298 us
    reduce_scatter x1, waiting for transfers between devices, on_device(): lax.psum_scatter(jnp.dot(block, gen_out_w, preferred_element_type=jnp.flo...  83.3 us
    psum x1, waiting for transfers between devices, on_device(): lax.psum((projected, partial_squares, shift_proj), 'mp')  67.8 us
    all_gather x1, waiting for transfers between devices, on_device(): gathered = lax.all_gather(noisy, 'seq', axis=0, tiled=True)  58.8 us
  transfers between devices with their start and end apart: 5, of which 5 were waited for; matrix products, arithmetic and copies ran while one was open for 2% of the time, Pallas kernels for 0%

commit v1 on v0

v1 whole, which is shorter than its diff:
```python
import math

import jax
import jax.numpy as jnp
from jax import lax
from jax.sharding import PartitionSpec as P

D = 5120
HEAD_DIM = 128
BF16 = jnp.bfloat16
F32 = jnp.float32


def time_embed(step_value, width):
    half_width = width // 2
    positions = jnp.arange(half_width, dtype=F32)
    frequencies = jnp.exp(positions * (-math.log(10000.0) / half_width))
    angles = step_value.astype(F32) * frequencies
    return jnp.concatenate([jnp.cos(angles), jnp.sin(angles)]).astype(BF16)


def head_norm(values, gains):
    factor = lax.rsqrt(jnp.mean(values * values, axis=-1, keepdims=True) + 1e-06)
    return (values * factor * gains).astype(BF16)


def dot(a, b):
    return jnp.dot(a, b, preferred_element_type=F32)


def on_device(
    gen_heads,
    gen_resid,
    gen_out_w,
    gen_time_w,
    noise,
    steps,
    teacher_qkv,
    teacher_out,
    teacher_time,
    teacher_norm,
    critic_qkv,
    critic_out,
    critic_time,
    critic_norm,
):
    role = lax.axis_index("role")
    mp = lax.axis_index("mp")
    embeds = jnp.stack([time_embed(steps[i], gen_time_w.shape[0]) for i in range(3)])
    gen_gate = dot(embeds[0:1], gen_time_w)[0]
    modulation = [
        jnp.einsum("lf,fkd->lkd", embeds[1:3], w, preferred_element_type=F32)
        for w in (teacher_time, critic_time)
    ]
    heads_r = lax.dynamic_index_in_dim(
        gen_heads.reshape(16, 4, 16, 256), role, 1, keepdims=False
    ).reshape(256, 256)
    gen_sum = lax.psum_scatter(
        dot(heads_r, gen_out_w).astype(BF16), "seq", scatter_dimension=0, tiled=True
    )
    resid_r = lax.dynamic_slice_in_dim(gen_resid, role * 16, 16, 0)
    noise_r = lax.dynamic_slice_in_dim(noise, role * 16, 16, 0)
    latent_r = (resid_r.astype(F32) + gen_gate * gen_sum.astype(F32)).astype(BF16)
    latent = lax.all_gather(latent_r, "role", axis=0, tiled=True)
    latent_all = lax.all_gather(latent_r, "seq", axis=0, tiled=True)
    noise_all = lax.all_gather(noise_r, "seq", axis=0, tiled=True)
    projected = [None] * 4
    shifts = [None] * 4
    squares = []
    for level in range(2):
        noise_level = steps[1 + level].astype(F32) / 1000.0
        noisy = (
            (1.0 - noise_level) * latent_all.astype(F32) + noise_level * noise_all.astype(F32)
        ).astype(BF16)
        squares.append(jnp.sum(jnp.square(noisy.astype(F32)), axis=1))
        for model, w in enumerate((teacher_qkv, critic_qkv)):
            mod = modulation[model][level]
            scaled = (noisy.astype(F32) * (1.0 + mod[1])).astype(BF16)
            p = 2 * level + model
            projected[p] = jnp.einsum(
                "td,dkc->tkc", scaled, w, preferred_element_type=F32
            ).astype(BF16)
            shifts[p] = jnp.einsum(
                "d,dkc->kc", mod[0].astype(BF16), w, preferred_element_type=F32
            )
    mine = lax.psum_scatter(
        jnp.stack(projected), "mp", scatter_dimension=0, tiled=False
    )
    squares, shifts = lax.psum((jnp.stack(squares), jnp.stack(shifts)), "mp")
    square = lax.dynamic_index_in_dim(squares, mp // 2, 0, keepdims=False)
    shift = lax.dynamic_index_in_dim(shifts, mp, 0, keepdims=False)
    mixed = mine.astype(F32) * lax.rsqrt(square / D + 1e-06)[:, None, None] + shift
    w_norm = jnp.where(mp % 2 == 1, critic_norm, teacher_norm)
    gains = w_norm.reshape(2, 2, HEAD_DIM)
    mixed = mixed.reshape(256, 3, 2, HEAD_DIM)
    query = head_norm(mixed[:, 0], gains[0])
    key = head_norm(mixed[:, 1], gains[1])
    value = mixed[:, 2].astype(BF16)
    kv = lax.all_gather(jnp.stack([key, value]), "role", axis=1, tiled=True)
    logits = jnp.einsum(
        "qhd,khd->hqk", query, kv[0], preferred_element_type=F32
    ) * (1.0 / math.sqrt(HEAD_DIM))
    expanded = jnp.exp(logits)
    probs = (expanded / jnp.sum(expanded, axis=2, keepdims=True)).astype(BF16)
    head_out = jnp.einsum(
        "hqk,khd->qhd", probs, kv[1], preferred_element_type=F32
    ).astype(BF16).reshape(256, 256)
    heads_all = lax.all_gather(head_out, "mp", axis=0, tiled=False)
    score = jnp.zeros((256, 1280), F32)
    for p in range(4):
        gate = modulation[p % 2][p // 2][2]
        out_w = (teacher_out, critic_out)[p % 2]
        score = score + (0.5 if p % 2 else -0.5) * gate * dot(heads_all[p], out_w)
    summed = lax.psum_scatter(score.astype(BF16), "seq", scatter_dimension=0, tiled=True)
    grad_r = (gen_gate * summed.astype(F32)).astype(BF16)
    grad_c = lax.all_to_all(
        grad_r.reshape(16, 4, 320), "role", split_axis=1, concat_axis=0, tiled=False
    ).reshape(64, 320)
    grad_rows = lax.all_gather(grad_c, "seq", axis=0, tiled=True)
    weight_grad = lax.dot_general(
        gen_heads, grad_rows, (((0,), (0,)), ((), ())), preferred_element_type=F32
    ).astype(BF16)
    weight_grad = lax.all_gather(weight_grad, "role", axis=1, tiled=True)
    return (latent, weight_grad)


def solution(mesh):
    in_specs = (
        P(None, "seq"),
        P("seq", "mp"),
        P("seq", "mp"),
        P(None, "mp"),
        P("seq", "mp"),
        P(),
        P("mp", None, "seq"),
        P("seq", "mp"),
        P(None, None, "mp"),
        P(None, "seq"),
        P("mp", None, "seq"),
        P("seq", "mp"),
        P(None, None, "mp"),
        P(None, "seq"),
    )
    out_specs = (P("seq", "mp"), P("seq", "mp"))
    return jax.shard_map(
        on_device, mesh=mesh, in_specs=in_specs, out_specs=out_specs, check_vma=False
    )
```

time: 910 us -> 355 us (0.39); the launches traced: 897 us -> 354 us
  waiting for transfers between devices: 821 us -> 143 us
  blocking collectives: 7.27 us -> 156 us
    all_gather x2 -> x1, waiting for transfers between devices: 357 us -> 27 us  [on_device(): kv = lax.all_gather(jnp.stack([key, value]), 'role', axis=1, tiled=True)]
    reduce_scatter x2 -> x3, waiting for transfers between devices: 396 us -> 115 us  [the longest x1 71.1 us: on_device(): lax.psum_scatter(score.astype(BF16), 'seq', scatter_dimension=0, tiled=True)]
    all_gather x0 -> x6, blocking collectives: none -> 143 us  [the longest x1 39.3 us: on_device(): noise_all = lax.all_gather(noise_r, 'seq', axis=0, tiled=True)]
    psum x1 -> x0, waiting for transfers between devices: 67.8 us -> none  [on_device(): lax.psum((projected, partial_squares, shift_proj), 'mp')]
    dot_general x8 -> x18, matrix products: 19.6 us -> 15.2 us  [the longest x6 4.74 us: dot(): return jnp.dot(a, b, preferred_element_type=F32)]
  transfers between devices with their start and end apart: 5 -> 5, of which waited for: 5 -> 4; matrix products, arithmetic and copies ran while one was open for 2% -> 3% of each run, Pallas kernels for 0% -> 0%
where the time goes in v1:
time: 355 us; the launch traced here: 354 us
  blocking collectives  156 us (44%)
  waiting for transfers between devices  143 us (40%)
  between operations  16 us (5%)
  matrix products  15.6 us (4%)
  local copies, waits for them, and re-layouts  11.1 us (3%)
  other arithmetic  8.51 us (2%)
  starting transfers between devices  4.46 us (1%)
    reduce_scatter x1, waiting for transfers between devices, on_device(): lax.psum_scatter(score.astype(BF16), 'seq', scatter_dimension=0, tiled=True)  71.1 us
    all_gather x1, blocking collectives, on_device(): noise_all = lax.all_gather(noise_r, 'seq', axis=0, tiled=True)  39.3 us
    all_gather x1, blocking collectives, on_device(): grad_rows = lax.all_gather(grad_c, 'seq', axis=0, tiled=True)  35 us
    all_gather x1, blocking collectives, on_device(): latent_all = lax.all_gather(latent_r, 'seq', axis=0, tiled=True)  34.3 us
    all_gather x1, waiting for transfers between devices, on_device(): kv = lax.all_gather(jnp.stack([key, value]), 'role', axis=1, tiled=True)  27 us
    reduce_scatter x1, waiting for transfers between devices, on_device(): lax.psum_scatter(dot(heads_r, gen_out_w).astype(BF16), 'seq', scatter_dim...  26 us
    reduce_scatter x1, waiting for transfers between devices, on_device(): lax.psum_scatter(jnp.stack(projected), 'mp', scatter_dimension=0, tiled=F...  18.4 us
    psum x1, blocking collectives, on_device(): squares, shifts = lax.psum((jnp.stack(squares), jnp.stack(shifts)), 'mp')  13.3 us
  transfers between devices with their start and end apart: 5, of which 4 were waited for; matrix products, arithmetic and copies ran while one was open for 3% of the time, Pallas kernels for 0%

profile of v1, /device:TPU:2, one launch (start us, length us, event | category | flops | bytes accessed | tf_op | source)
XLA Modules:
  0.0 354.1 jit_solution(8491889341987475081)
XLA Ops:
  7.2 1.1 constant_dynamic-slice_fusion.3
  8.3 2.3 convolution_convert_fusion
  13.3 1.9 fusion.62
  16.0 1.9 fusion.61
  18.8 0.8 constant_dynamic-slice_fusion.2
  19.6 39.3 %all_gather.23 = bf16[256,1280]{1,0:T(8,128)(2,1)S(1)} all-gather(bf16[16,1280]{1,0:T(8,128)(2,1)S(1)} %constant_dynamic-slice_fusion.2), channel_id=1, replica_groups=mesh['role'=4,'seq'=16,'mp'=4] {'seq'}, dimensions={0}, use_global_device_ids=true | all-gather | bytes 696320 | tf_op jit(solution)/shard_map/all_gather | solution.py:66
  58.9 26.0 %reduce-scatter.4.cloned.1.call-done = bf16[16,1280]{1,0:T(8,128)(2,1)} async-done(((bf16[256,1280]{1,0:T(8,128)(2,1)}), bf16[16,1280]{1,0:T(8,128)(2,1)}) %reduce-scatter.4.cloned.1.call-update) | async-done | bytes 40976 | tf_op jit(solution)/shard_map/reduce_scatter | solution.py:58
  85.0 0.8 add_convert_fusion
  86.4 34.3 %all_gather.22 = bf16[256,1280]{1,0:T(8,128)(2,1)S(1)} all-gather(bf16[16,1280]{1,0:T(8,128)(2,1)S(1)} %add_convert_fusion), channel_id=1, replica_groups=mesh['role'=4,'seq'=16,'mp'=4] {'seq'}, dimensions={0}, use_global_device_ids=true | all-gather | bytes 696320 | tf_op jit(solution)/shard_map/all_gather | solution.py:65
  120.7 0.8 fusion.11
  122.2 0.8 copy-done.1
  123.8 0.7 fusion.17
  125.2 1.4 pad_maximum_fusion
  127.0 1.2 copy-done.2
  130.0 13.3 %all-reduce = (f32[4,3,256]{2,1,0:T(4,128)S(1)}, f32[2,256]{1,0:T(2,128)S(1)}) all-reduce(f32[4,3,256]{2,1,0:T(4,128)S(1)} %pad_maximum_fusion.2, f32[2,256]{1,0:T(2,128)S(1)} %pad_maximum_fusion.3), channel_id=1, replica_groups=mesh['role'=4,'seq'=16,'mp'=4] {'mp'}, use_global_device_ids=true, to_apply=%region_5.6 | all-reduce | flops 3584 | bytes 28672 | tf_op jit(solution)/shard_map/psum | solution.py:89
  144.4 18.4 %reduce-scatter.6.cloned.1.call-done = bf16[1,256,3,256]{3,1,2,0:T(8,128)(2,1)} async-done(((bf16[4,256,3,256]{3,1,2,0:T(8,128)(2,1)}), bf16[1,256,3,256]{3,1,2,0:T(8,128)(2,1)}) %reduce-scatter.6.cloned.1.call-update) | async-done | bytes 393232 | tf_op jit(solution)/shard_map/reduce_scatter | solution.py:86
  162.8 1.4 reshape.228
  164.2 0.8 fusion.20
  165.2 0.8 fusion.35
  166.0 0.7 pad_maximum_fusion.1
  167.0 27.0 %all-gather.2.cloned.1.call-done = bf16[2,1024,2,128]{3,1,2,0:T(8,128)(2,1)} async-done(((bf16[2,256,2,128]{3,1,2,0:T(8,128)(2,1)}), bf16[2,1024,2,128]{3,1,2,0:T(8,128)(2,1)}) %all-gather.2.cloned.1.call-update) | async-done | bytes 1048592 | tf_op jit(solution)/shard_map/all_gather | solution.py:99
  194.0 1.7 fusion.4
  196.5 8.0 %all_gather.25 = bf16[4,256,256]{2,1,0:T(8,128)(2,1)S(1)} all-gather(bf16[1,256,256]{2,1,0:T(8,128)(2,1)S(1)} %copy.25), channel_id=1, replica_groups=mesh['role'=4,'seq'=16,'mp'=4] {'mp'}, dimensions={0}, use_global_device_ids=true | all-gather | bytes 655360 | tf_op jit(solution)/shard_map/all_gather | solution.py:108
  205.2 0.7 copy-done.4
  206.3 1.2 fusion.3
  207.5 71.1 %reduce-scatter.8.cloned.1.call-done = bf16[16,1280]{1,0:T(8,128)(2,1)} async-done(((bf16[256,1280]{1,0:T(8,128)(2,1)}), bf16[16,1280]{1,0:T(8,128)(2,1)}) %reduce-scatter.8.cloned.1.call-update) | async-done | bytes 40976 | tf_op jit(solution)/shard_map/reduce_scatter | solution.py:114
  278.6 0.8 multiply_convert_fusion.2
  280.2 4.3 %all-to-all-start = ((bf16[1,16,4,320]{3,1,0,2:T(8,128)(2,1)}), bf16[1,16,4,320]{3,1,0,2:T(8,128)(2,1)S(1)}, u32[]{:S(2)}, u32[]{:S(2)}) async-start(bf16[1,16,4,320]{3,1,0,2:T(8,128)(2,1)} %copy.26), calls=%async_computation.3 | async-start | bytes 98304 | tf_op jit(solution)/shard_map/all_to_all | solution.py:116
  284.5 12.9 %all_gather.21 = bf16[64,1280]{1,0:T(8,128)(2,1)S(1)} all-gather(bf16[16,1280]{1,0:T(8,128)(2,1)S(1)} %copy-done.7), channel_id=1, replica_groups=mesh['role'=4,'seq'=16,'mp'=4] {'role'}, dimensions={0}, use_global_device_ids=true | all-gather | bytes 204800 | tf_op jit(solution)/shard_map/all_gather | solution.py:64
  297.4 35.0 %all_gather.26 = bf16[1024,320]{1,0:T(8,128)(2,1)S(1)} all-gather(bf16[64,320]{1,0:T(8,128)(2,1)S(1)} %bitcast.134), channel_id=1, replica_groups=mesh['role'=4,'seq'=16,'mp'=4] {'seq'}, dimensions={0}, use_global_device_ids=true | all-gather | bytes 696320 | tf_op jit(solution)/shard_map/all_gather | solution.py:119
  332.8 13.0 %all_gather.27 = bf16[256,1280]{0,1:T(8,128)(2,1)S(1)} all-gather(bf16[256,320]{0,1:T(8,128)(2,1)S(1)} %fusion.19), channel_id=1, replica_groups=mesh['role'=4,'seq'=16,'mp'=4] {'role'}, dimensions={1}, use_global_device_ids=true | all-gather | bytes 819200 | tf_op jit(solution)/shard_map/all_gather | solution.py:123
  345.8 1.1 copy.27
  (81 shorter events, 12.6 us)
Async XLA Ops:
  7.2 114.4 %copy-start = (bf16[1280,3,256]{2,0,1:T(8,128)(2,1)S(1)}, bf16[1280,3,256]{2,0,1:T(8,128)(2,1)}, u32[]{:S(2)}) copy-start(bf16[1280,3,256]{2,0,1:T(8,128)(2,1)} %param.20) | copy-start | bytes 5898244
  7.2 3.5 copy-start.13
  7.2 77.8 %reduce-scatter.4.cloned.1.call-start = ((), (), s32[]{:S(2)}) async-start(), calls=%async_computation.4 | async-start | bytes 696320 | tf_op jit(solution)/shard_map/reduce_scatter | solution.py:58
  10.6 152.2 %reduce-scatter.6.cloned.1.call-start = ((), (), s32[]{:S(2)}) async-start(), calls=%async_computation.5 | async-start | bytes 1966080 | tf_op jit(solution)/shard_map/reduce_scatter | solution.py:86
  15.2 3.3 copy-start.5
  85.8 0.6 copy-start.6
  121.5 1.5 copy-start.1
  126.6 67.4 %all-gather.2.cloned.1.call-start = ((), (), s32[]{:S(2)}) async-start(), calls=%async_computation.6 | async-start | bytes 1310720 | tf_op jit(solution)/shard_map/all_gather | solution.py:99
  126.6 1.5 copy-start.2
  128.5 0.8 copy-start.15
  128.5 0.8 copy-start.16
  165.0 29.0 %copy-start.14 = (f32[1,256]{1,0:T(1,128)S(1)}, f32[1,256]{1,0:T(1,128)}, u32[]{:S(2)}) copy-start(f32[1,256]{1,0:T(1,128)} %get-tuple-element.24) | copy-start | bytes 3076
  166.8 111.8 %reduce-scatter.8.cloned.1.call-start = ((), (), s32[]{:S(2)}) async-start(), calls=%async_computation.7 | async-start | bytes 696320 | tf_op jit(solution)/shard_map/reduce_scatter | solution.py:114
  194.0 1.7 copy-start.8
  195.7 8.8 %copy-start.3 = (bf16[256,1280]{1,0:T(8,128)(2,1)S(1)}, bf16[256,1280]{1,0:T(8,128)(2,1)}, u32[]{:S(2)}) copy-start(bf16[256,1280]{1,0:T(8,128)(2,1)} %param.25) | copy-start | bytes 1966084
  195.7 8.8 %copy-start.11 = (f32[1280]{0:T(1024)S(1)}, f32[1280]{0:T(1024)}, u32[]{:S(2)}) copy-start(f32[1280]{0:T(1024)} %get-tuple-element.12) | copy-start | bytes 15364
  196.4 8.5 %copy-start.10 = (f32[1280]{0:T(1024)S(1)}, f32[1280]{0:T(1024)}, u32[]{:S(2)}) copy-start(f32[1280]{0:T(1024)} %get-tuple-element.13) | copy-start | bytes 15364
  204.8 1.1 copy-start.4
  204.8 1.1 copy-start.9
  206.3 78.2 %copy-start.7 = (bf16[16,1280]{1,0:T(8,128)(2,1)S(1)}, bf16[16,1280]{1,0:T(8,128)(2,1)}, u32[]{:S(2)}) copy-start(bf16[16,1280]{1,0:T(8,128)(2,1)} %copy-done.6) | copy-start | bytes 122884
  207.5 124.9 %copy-start.12 = (bf16[1024,256]{1,0:T(8,128)(2,1)S(1)}, bf16[1024,256]{1,0:T(8,128)(2,1)}, u32[]{:S(2)}) copy-start(bf16[1024,256]{1,0:T(8,128)(2,1)} %param.14) | copy-start | bytes 1572868
  280.2 17.2 %all-to-all-start = ((bf16[1,16,4,320]{3,1,0,2:T(8,128)(2,1)}), bf16[1,16,4,320]{3,1,0,2:T(8,128)(2,1)S(1)}, u32[]{:S(2)}, u32[]{:S(2)}) async-start(bf16[1,16,4,320]{3,1,0,2:T(8,128)(2,1)} %copy.26), calls=%async_computation.3 | async-start | bytes 98304 | tf_op jit(solution)/shard_map/all_to_all | solution.py:116
Sparse Core Ops, SparseCore 0:
  11.1 73.8 reduce-scatter.3
  126.7 36.0 reduce-scatter.5
  166.9 27.0 all-gather.1
  207.6 70.9 reduce-scatter.7

commit v2 on v1

v2 whole, which is shorter than its diff:
```python
import math

import jax
import jax.numpy as jnp
from jax import lax
from jax.experimental import pallas as pl
from jax.experimental.pallas import tpu as pltpu
from jax.sharding import PartitionSpec as P

D = 5120
HEAD_DIM = 128
BF16 = jnp.bfloat16
F32 = jnp.float32
MESH = pl.DeviceIdType.MESH
FAR_FIRST = (4, 3, 5, 2, 6, 1, 7)


def time_embed(step_value, width):
    half_width = width // 2
    positions = jnp.arange(half_width, dtype=F32)
    frequencies = jnp.exp(positions * (-math.log(10000.0) / half_width))
    angles = step_value.astype(F32) * frequencies
    return jnp.concatenate([jnp.cos(angles), jnp.sin(angles)]).astype(BF16)


def dot(a, b):
    return jnp.dot(a, b, preferred_element_type=F32)


def dot_t(a, b):
    return lax.dot_general(a, b, (((1,), (1,)), ((), ())), preferred_element_type=F32)


def column_start(role):
    return pl.multiple_of((2 * role + (role + 3) // 4) * 128, 128)


def kernel(
    gh4, resid4, gow, gtw, noise4, emb, lv, tq, cq, tow, cow, ttw, ctw, norms,
    latent_out, grad_out,
    heads_r, heads, ow_gen, tw_gen, resid, wq, ow, tw, nrm, gg, md,
    p1b, p1f, x1r, z1s, z1r, la, na, lat4,
    sc, sqc, sqs, cqr, sqx, xqr,
    cs, cr, of, xs, xr, kvb, qb, hos, ha,
    acc, p2b, x2r, z2s, z2r, grad, ga, wga,
    lsem,
    n_zs, n_zr, n_xs, n_xr,
    a_xs, a_xr, a_zs, a_zr,
    l_zs, l_zr, l_xs, l_xr, l_ys, l_yr,
    b_xs, b_xr, b_zs, b_zr,
    g_ys, g_yr, g_zs, g_zr, g_xs, g_xr,
    m_s, m_r, q_s, q_r, c_s, c_r, x_s, x_r,
    kv_s, kv_r, h_s, h_r, w_s, w_r,
):
    r = lax.axis_index("role")
    s = lax.axis_index("seq")
    m = lax.axis_index("mp")
    xl, z = s // 8, lax.rem(s, 8)
    xh, c = m // 2, lax.rem(m, 2)
    ol = 1 - xl
    oc = 1 - c
    z_of = lambda dz: lax.rem(z + dz, 8)
    z_dev = lambda dz: {"seq": xl * 8 + z_of(dz)}
    x_dev = {"seq": ol * 8 + z}
    core_dev = {"mp": 2 * xh + oc}
    side_dev = lambda level: {"seq": ol * 8 + z, "mp": 2 * level + c}
    y_of = lambda d: lax.rem(r + d, 4)
    y_dev = lambda d: {"role": y_of(d)}

    def rc(src, dst, ssem, rsem, dev):
        return pltpu.make_async_remote_copy(
            src_ref=src, dst_ref=dst, send_sem=ssem, recv_sem=rsem,
            device_id=dev, device_id_type=MESH,
        )

    sent = []

    def send(*args):
        copy = rc(*args)
        copy.start()
        sent.append(copy)

    def got(dst, rsem):
        rc(dst, dst, rsem, rsem, x_dev).wait_recv()

    loads = []

    def load(src, dst):
        copy = pltpu.make_async_copy(src, dst, lsem.at[len(loads)])
        copy.start()
        loads.append(copy)
        return copy

    barrier = pltpu.get_barrier_semaphore()
    peers = [z_dev(dz) for dz in range(1, 8)] + [x_dev, core_dev]
    peers += [side_dev(1 - xh)] + [y_dev(d) for d in (1, 2, 3)]
    for dev in peers:
        pl.semaphore_signal(barrier, inc=1, device_id=dev, device_id_type=MESH)
    l_heads = load(gh4.at[:, r], heads_r)
    l_gow = load(gow, ow_gen)
    l_noise = load(noise4.at[r], na.at[s])
    l_resid = load(resid4.at[r], resid)
    l_gtw = load(gtw, tw_gen)
    l_tt = load(ttw, tw.at[0])
    l_ct = load(ctw, tw.at[1])
    l_tq = load(tq, wq.at[0])
    l_cq = load(cq, wq.at[1])
    l_to = load(tow, ow.at[0])
    l_co = load(cow, ow.at[1])
    l_all = load(gh4, heads)
    l_heads.wait()
    l_gow.wait()
    l_noise.wait()
    part = dot(heads_r[pl.ds(ol * 8, 8)].reshape(128, 256), ow_gen[...])
    p1b[...] = part.astype(BF16).reshape(8, 16, 1280)
    pl.semaphore_wait(barrier, len(peers))

    for dz in FAR_FIRST:
        send(na.at[s], na.at[s], n_zs.at[dz], n_zr.at[z], z_dev(dz))
    send(norms, nrm, m_s, m_r, x_dev)

    def sum_start(pb, xr_buf, xs_sem, xr_sem):
        for dz in FAR_FIRST + (0,):
            zz = z_of(dz)
            send(pb.at[zz], xr_buf.at[zz], xs_sem.at[zz], xr_sem.at[zz], x_dev)

    def sum_middle(pf, xr_buf, xr_sem, zs_buf, zr_buf, zs_sem, zr_sem):
        for dz in FAR_FIRST:
            zz = z_of(dz)
            got(xr_buf.at[zz], xr_sem.at[zz])
            zs_buf[zz] = (pf[zz] + xr_buf[zz].astype(F32)).astype(BF16)
            send(zs_buf.at[zz], zr_buf.at[z], zs_sem.at[dz], zr_sem.at[z], z_dev(dz))

    def sum_end(pf, xr_buf, xr_sem, zr_buf, zr_sem):
        got(xr_buf.at[z], xr_sem.at[z])
        total = pf[z] + xr_buf[z].astype(F32)
        for dz in reversed(FAR_FIRST):
            zz = z_of(dz)
            got(zr_buf.at[zz], zr_sem.at[zz])
            total = total + zr_buf[zz].astype(F32)
        return total

    sum_start(p1b, x1r, a_xs, a_xr)
    p1f[...] = dot(heads_r[pl.ds(xl * 8, 8)].reshape(128, 256), ow_gen[...]).reshape(8, 16, 1280)
    sum_middle(p1f, x1r, a_xr, z1s, z1r, a_zs, a_zr)
    send(na.at[s], na.at[s], n_xs.at[z], n_xr.at[z], x_dev)
    for dz in reversed(FAR_FIRST):
        zz = z_of(dz)
        got(na.at[xl * 8 + zz], n_zr.at[zz])
        send(na.at[xl * 8 + zz], na.at[xl * 8 + zz], n_xs.at[zz], n_xr.at[zz], x_dev)

    l_gtw.wait()
    gg[...] = dot(emb[...], tw_gen[...])
    l_tt.wait()
    l_ct.wait()

    def modulate(i, carry):
        md[i // 3, lax.rem(i, 3)] = dot(emb[...], tw[i // 3, lax.rem(i, 3)])
        return carry

    lax.fori_loop(0, 6, modulate, 0)
    l_resid.wait()

    total = sum_end(p1f, x1r, a_xr, z1r, a_zr)
    latent = (resid[...].astype(F32) + gg[0:1, :] * total).astype(BF16)
    la[s] = latent
    lat4[r] = latent

    for dz in FAR_FIRST:
        send(la.at[s], la.at[s], l_zs.at[dz], l_zr.at[z], z_dev(dz))
    send(la.at[s], la.at[s], l_xs.at[z], l_xr.at[z], x_dev)
    for d in (1, 2, 3):
        send(lat4.at[r], lat4.at[r], l_ys.at[d], l_yr.at[r], y_dev(d))
    for level in range(2):
        for model in range(2):
            first = lax.broadcasted_iota(jnp.int32, (16, 1280), 0) == 0
            shift = md[model, 0, 1 + level : 2 + level, :]
            sc[level, model, 256:272, :] = jnp.where(first, shift, 0.0).astype(BF16)

    def prepare(b):
        rows = pl.ds(pl.multiple_of(b * 16, 16), 16)
        lat = la[b].astype(F32)
        noi = na[b].astype(F32)
        for level in range(2):
            sl = lv[level : level + 1, 0:1]
            noisy = ((1.0 - sl) * lat + sl * noi).astype(BF16).astype(F32)
            square = jnp.sum(noisy * noisy, axis=1, keepdims=True)
            sqc[level, rows, :] = jnp.broadcast_to(square, (16, 128))
            for model in range(2):
                scale = 1.0 + md[model, 1, 1 + level : 2 + level, :]
                sc[level, model, rows, :] = (noisy * scale).astype(BF16)

    prepare(s)
    for dz in reversed(FAR_FIRST):
        zz = z_of(dz)
        b = xl * 8 + zz
        got(la.at[b], l_zr.at[zz])
        send(la.at[b], la.at[b], l_xs.at[zz], l_xr.at[zz], x_dev)
        prepare(b)
    for dz in (0,) + tuple(reversed(FAR_FIRST)):
        zz = z_of(dz)
        b = ol * 8 + zz
        got(la.at[b], l_xr.at[zz])
        got(na.at[b], n_xr.at[zz])
        prepare(b)

    l_tq.wait()
    l_cq.wait()

    def qkv_dots(k):
        kind = (k + 1) % 3
        for level in range(2):
            cs[k, level] = dot(sc[level, oc], wq[oc, kind]).astype(BF16)
            send(cs.at[k, level], cr.at[k, level], c_s.at[k, level], c_r.at[k, level], core_dev)
        for level in range(2):
            of[k % 2, level] = dot(sc[level, c], wq[c, kind])

    def qkv_sums(k):
        for level in range(2):
            got(cr.at[k, level], c_r.at[k, level])
            xs[k, level] = (of[k % 2, level] + cr[k, level].astype(F32)).astype(BF16)
            send(xs.at[k, level], xr.at[k, xh], x_s.at[k, level], x_r.at[k, xh], side_dev(level))

    for level in range(2):
        row = jnp.transpose(sqc[level])[0:8, :]
        sqs[level] = row
    send(sqs, cqr, q_s.at[0], q_r.at[0], core_dev)
    qkv_dots(0)
    got(cqr, q_r.at[0])
    sqx[...] = sqs[...] + cqr[...]
    for level in range(2):
        send(sqx.at[level], xqr.at[xh], q_s.at[1 + level], q_r.at[1 + xh], side_dev(level))
    qkv_dots(1)
    qkv_sums(0)
    qkv_dots(2)
    qkv_sums(1)
    qkv_sums(2)

    for i in range(2):
        got(xqr.at[i], q_r.at[1 + i])
    square = jnp.broadcast_to((xqr[0] + xqr[1])[0:1, :], (128, 256))
    rinv = lax.rsqrt(jnp.transpose(square) * (1.0 / D) + 1e-06)
    got(nrm, m_r)

    def mixed_head(k, h):
        cols = slice(h * 128, h * 128 + 128)
        both = xr[k, 0, :, cols].astype(F32) + xr[k, 1, :, cols].astype(F32)
        return both[0:256] * rinv + both[256:257]

    def normed(values, gains):
        factor = lax.rsqrt(jnp.mean(values * values, axis=-1, keepdims=True) + 1e-06)
        return (values * factor * gains).astype(BF16)

    for k in range(2):
        for i in range(2):
            got(xr.at[k, i], x_r.at[k, i])
        for h in range(2):
            cols = slice(h * 128, h * 128 + 128)
            values = mixed_head(k, h)
            if k == 0:
                values = normed(values, nrm[c, 1:2, cols])
            kvb[k, r, :, cols] = values.astype(BF16)
        for d in (1, 3):
            send(kvb.at[k, r], kvb.at[k, r], kv_s.at[k, d], kv_r.at[k, r], y_dev(d))
    for i in range(2):
        got(xr.at[2, i], x_r.at[2, i])
    for h in range(2):
        cols = slice(h * 128, h * 128 + 128)
        qb[h] = normed(mixed_head(2, h), nrm[c, 0:1, cols])
    below, above, across = y_of(3), y_of(1), y_of(2)
    got(kvb.at[0, below], kv_r.at[0, below])
    send(kvb.at[0, below], kvb.at[0, below], kv_s.at[0, 2], kv_r.at[0, below], y_dev(1))
    got(kvb.at[0, above], kv_r.at[0, above])
    got(kvb.at[1, above], kv_r.at[1, above])
    send(kvb.at[1, above], kvb.at[1, above], kv_s.at[1, 2], kv_r.at[1, above], y_dev(3))

    exponent = math.log2(math.e) / math.sqrt(HEAD_DIM)
    sums = [jnp.zeros((256, 1), F32)] * 2
    outs = [jnp.zeros((256, 128), F32)] * 2
    for n, b in enumerate((r, above, below, across)):
        if n == 2:
            got(kvb.at[1, below], kv_r.at[1, below])
        if n == 3:
            got(kvb.at[0, across], kv_r.at[0, across])
            got(kvb.at[1, across], kv_r.at[1, across])
        for h in range(2):
            cols = slice(h * 128, h * 128 + 128)
            e = jnp.exp2(dot_t(qb[h], kvb[0, b, :, cols]) * exponent)
            sums[h] = sums[h] + jnp.sum(e, axis=1, keepdims=True)
            outs[h] = outs[h] + dot(e.astype(BF16), kvb[1, b, :, cols])
    for h in range(2):
        hos[:, h * 128 : h * 128 + 128] = (outs[h] / sums[h]).astype(BF16)
    for level in range(2):
        send(hos, ha.at[xh, c], h_s.at[level], h_r.at[xh, c], side_dev(level))

    l_to.wait()
    l_co.wait()

    def out_term(level, model, half):
        sign = (model.astype(F32) - 0.5) * md[model, 2, 1 + level : 2 + level, :]
        return sign * dot(ha[level, model, pl.ds(pl.multiple_of(half * 128, 128), 128)], ow[model])

    for level in range(2):
        got(ha.at[level, c], h_r.at[level, c])
        send(ha.at[level, c], ha.at[level, c], h_s.at[2 + level], h_r.at[level, c], core_dev)
    for half in range(2):
        acc[half] = out_term(0, c, half) + out_term(1, c, half)
    for level in range(2):
        got(ha.at[level, oc], h_r.at[level, oc])
    p2b[...] = (acc[ol] + out_term(0, oc, ol) + out_term(1, oc, ol)).astype(BF16).reshape(8, 16, 1280)
    sum_start(p2b, x2r, b_xs, b_xr)
    p1f[...] = (acc[xl] + out_term(0, oc, xl) + out_term(1, oc, xl)).reshape(8, 16, 1280)
    sum_middle(p1f, x2r, b_xr, z2s, z2r, b_zs, b_zr)
    for d in (1, 2, 3):
        got(lat4.at[y_of(d)], l_yr.at[y_of(d)])
    latent_out[...] = lat4[...].reshape(64, 1280)
    total = sum_end(p1f, x2r, b_xr, z2r, b_zr)
    grad[...] = (gg[0:1, :] * total).astype(BF16)

    for d in (2, 1, 3):
        src = grad.at[:, pl.ds(column_start(y_of(d)), 384)]
        send(src, ga.at[s, r], g_ys.at[d], g_yr.at[r], y_dev(d))
    ga[s, r] = grad[:, pl.ds(column_start(r), 384)]
    for d in (1, 3, 2):
        got(ga.at[s, y_of(d)], g_yr.at[y_of(d)])
    for dz in FAR_FIRST:
        send(ga.at[s], ga.at[s], g_zs.at[dz], g_zr.at[z], z_dev(dz))
    send(ga.at[s], ga.at[s], g_xs.at[z], g_xr.at[z], x_dev)
    for dz in reversed(FAR_FIRST):
        zz = z_of(dz)
        b = xl * 8 + zz
        got(ga.at[b], g_zr.at[zz])
        send(ga.at[b], ga.at[b], g_xs.at[zz], g_xr.at[zz], x_dev)
    l_all.wait()

    def grad_term(half):
        lhs = heads[pl.ds(half * 8, 8)].reshape(512, 256)
        rhs = ga[pl.ds(half * 8, 8)].reshape(512, 384)
        return lax.dot_general(lhs, rhs, (((0,), (0,)), ((), ())), preferred_element_type=F32)

    first_half = grad_term(xl)
    for dz in range(8):
        zz = z_of(dz)
        got(ga.at[ol * 8 + zz], g_xr.at[zz])
    wga[r] = (first_half + grad_term(ol)).astype(BF16).reshape(2, 128, 384)
    for i, d in ((0, 1), (1, 3), (1, 1), (0, 3)):
        send(wga.at[r, i], wga.at[r, i], w_s.at[i, d], w_r.at[i, r], y_dev(d))
    got(wga.at[below, 0], w_r.at[0, below])
    send(wga.at[below, 0], wga.at[below, 0], w_s.at[0, 2], w_r.at[0, below], y_dev(1))
    got(wga.at[above, 1], w_r.at[1, above])
    send(wga.at[above, 1], wga.at[above, 1], w_s.at[1, 2], w_r.at[1, above], y_dev(3))
    got(wga.at[below, 1], w_r.at[1, below])
    got(wga.at[above, 0], w_r.at[0, above])
    got(wga.at[across, 0], w_r.at[0, across])
    got(wga.at[across, 1], w_r.at[1, across])
    for i in range(2):
        rows = slice(i * 128, i * 128 + 128)
        grad_out[rows, 0:384] = wga[0, i]
        grad_out[rows, 384:768] = wga[1, i]
        grad_out[rows, 768:1024] = wga[2, i, :, 128:384]
        grad_out[rows, 1024:1280] = wga[3, i, :, 128:384]
    for copy in sent:
        copy.wait_send()


def on_device(
    gen_heads,
    gen_resid,
    gen_out_w,
    gen_time_w,
    noise,
    steps,
    teacher_qkv,
    teacher_out,
    teacher_time,
    teacher_norm,
    critic_qkv,
    critic_out,
    critic_time,
    critic_norm,
):
    embeds = jnp.stack([time_embed(steps[min(i, 2)], gen_time_w.shape[0]) for i in range(8)])
    levels = jnp.broadcast_to(
        jnp.pad(steps[1:3].astype(F32) / 1000.0, (0, 6))[:, None], (8, 128)
    )
    norms = jnp.stack([teacher_norm, critic_norm])
    vmem = pl.BlockSpec(memory_space=pltpu.VMEM)
    hbm = pl.BlockSpec(memory_space=pl.ANY)
    V = pltpu.VMEM
    S = pltpu.SemaphoreType.DMA
    block = (16, 1280)
    scratch = [
        V((16, 16, 256), BF16), V((16, 4, 16, 256), BF16), V((256, 1280), BF16),
        V((256, 1280), BF16), V(block, BF16), V((2, 3, 1280, 256), BF16),
        V((2, 256, 1280), BF16), V((2, 3, 256, 1280), BF16), V((2, 2, 256), F32),
        V((8, 1280), F32), V((2, 3, 8, 1280), F32),
        V((8,) + block, BF16), V((8,) + block, F32), V((8,) + block, BF16),
        V((8,) + block, BF16), V((8,) + block, BF16),
        V((16,) + block, BF16), V((16,) + block, BF16), V((4,) + block, BF16),
        V((2, 2, 272, 1280), BF16), V((2, 256, 128), F32),
        V((2, 8, 256), F32), V((2, 8, 256), F32), V((2, 8, 256), F32), V((2, 8, 256), F32),
        V((3, 2, 272, 256), BF16), V((3, 2, 272, 256), BF16), V((2, 2, 272, 256), F32),
        V((3, 2, 272, 256), BF16), V((3, 2, 272, 256), BF16),
        V((2, 4, 256, 256), BF16), V((2, 256, 128), BF16), V((256, 256), BF16),
        V((2, 2, 256, 256), BF16),
        V((2, 128, 1280), F32), V((8,) + block, BF16), V((8,) + block, BF16),
        V((8,) + block, BF16), V((8,) + block, BF16),
        V(block, BF16), V((16, 4, 16, 384), BF16), V((4, 2, 128, 384), BF16),
        S((12,)),
        S((8,)), S((8,)), S((8,)), S((8,)),
        S((8,)), S((8,)), S((8,)), S((8,)),
        S((8,)), S((8,)), S((8,)), S((8,)), S((4,)), S((4,)),
        S((8,)), S((8,)), S((8,)), S((8,)),
        S((4,)), S((4,)), S((8,)), S((8,)), S((8,)), S((8,)),
        S(()), S(()), S((3,)), S((3,)), S((3, 2)), S((3, 2)), S((3, 2)), S((3, 2)),
        S((2, 4)), S((2, 4)), S((4,)), S((2, 2)), S((2, 4)), S((2, 4)),
    ]
    latent, weight_grad = pl.pallas_call(
        kernel,
        out_shape=(
            jax.ShapeDtypeStruct((64, 1280), BF16),
            jax.ShapeDtypeStruct((256, 1280), BF16),
        ),
        in_specs=[hbm] * 5 + [vmem] * 2 + [hbm] * 6 + [vmem],
        out_specs=(vmem, vmem),
        scratch_shapes=scratch,
        compiler_params=pltpu.CompilerParams(
            collective_id=0, has_side_effects=True, vmem_limit_bytes=60 * 1024 * 1024
        ),
        name="step",
    )(
        gen_heads.reshape(16, 4, 16, 256),
        gen_resid.reshape(4, 16, 1280),
        gen_out_w,
        gen_time_w,
        noise.reshape(4, 16, 1280),
        embeds,
        levels,
        teacher_qkv.transpose(1, 0, 2),
        critic_qkv.transpose(1, 0, 2),
        teacher_out,
        critic_out,
        teacher_time.transpose(1, 0, 2),
        critic_time.transpose(1, 0, 2),
        norms,
    )
    return (latent, weight_grad)


def solution(mesh):
    in_specs = (
        P(None, "seq"),
        P("seq", "mp"),
        P("seq", "mp"),
        P(None, "mp"),
        P("seq", "mp"),
        P(),
        P("mp", None, "seq"),
        P("seq", "mp"),
        P(None, None, "mp"),
        P(None, "seq"),
        P("mp", None, "seq"),
        P("seq", "mp"),
        P(None, None, "mp"),
        P(None, "seq"),
    )
    out_specs = (P("seq", "mp"), P("seq", "mp"))
    return jax.shard_map(
        on_device, mesh=mesh, in_specs=in_specs, out_specs=out_specs, check_vma=False
    )
```

time: 355 us -> 128 us (0.36)
  blocking collectives: 156 us -> 0 us
  waiting for transfers between devices: 143 us -> 0 us
  Pallas kernels: 0 us -> 116 us
  matrix products: 15.6 us -> 0 us
  between operations: 16 us -> 2.54 us
  other arithmetic: 8.51 us -> 2.2 us
  local copies, waits for them, and re-layouts: 11.1 us -> 6.2 us
  starting transfers between devices: 4.46 us -> 0 us
    all_gather x6 -> x0, blocking collectives: 143 us -> none  [the longest x1 39.3 us: on_device(): noise_all = lax.all_gather(noise_r, 'seq', axis=0, tiled=True)]
    pallas_call x0 -> x1, Pallas kernels: none -> 116 us  [on_device(): pl.pallas_call(kernel, out_shape=(jax.ShapeDtypeStruct((64, 1280), BF16),...]
    reduce_scatter x3 -> x0, waiting for transfers between devices: 115 us -> none  [the longest x1 71.1 us: on_device(): lax.psum_scatter(score.astype(BF16), 'seq', scatter_dimension=0, tiled=True)]
    all_gather x1 -> x0, waiting for transfers between devices: 27 us -> none  [on_device(): kv = lax.all_gather(jnp.stack([key, value]), 'role', axis=1, tiled=True)]
    dot_general x19 -> x0, matrix products: 15.6 us -> none  [the longest x6 4.74 us: dot(): return jnp.dot(a, b, preferred_element_type=F32)]
    psum x1 -> x0, blocking collectives: 13.3 us -> none  [on_device(): squares, shifts = lax.psum((jnp.stack(squares), jnp.stack(shifts)), 'mp')]
    all_to_all x1 -> x0, starting transfers between devices: 4.3 us -> none  [on_device(): lax.all_to_all(grad_r.reshape(16, 4, 320), 'role', split_axis=1, concat_a...]
  transfers between devices with their start and end apart: 5 -> 0, of which waited for: 4 -> 0; matrix products, arithmetic and copies ran while one was open for 3% -> 0% of each run, Pallas kernels for 0% -> 0%
where the time goes in v2:
time: 128 us; the launch traced here: 127 us
  Pallas kernels  116 us (91%)
  local copies, waits for them, and re-layouts  6.2 us (5%)
  between operations  2.54 us (2%)
  other arithmetic  2.2 us (2%)
    pallas_call x1, Pallas kernels, on_device(): pl.pallas_call(kernel, out_shape=(jax.ShapeDtypeStruct((64, 1280), BF16),...  116 us
    unnamed x2, local copies, waits for them, and re-layouts  3.56 us

profile of v2, /device:TPU:2, one launch (start us, length us, event | category | flops | bytes accessed | tf_op | source)
XLA Modules:
  0.0 126.9 jit_solution(14970107417958922335)
XLA Ops:
  0.6 0.7 convert_multiply_fusion
  1.4 1.4 %fusion = (s32[1]{0:T(128)}, s32[1]{0:T(128)}, s32[1]{0:T(128)}) fusion(s32[3]{0:T(128)} %param.19), kind=kLoop, calls=%fused_computation.12 | loop fusion | bytes 24 | tf_op jit(solution)/shard_map/slice | solution.py:382
  4.6 0.1 convert_bitcast_fusion
  4.7 0.1 convert_bitcast_fusion.2
  4.7 0.1 convert_bitcast_fusion.4
  4.8 0.6 stack.8.emb
  5.4 0.7 broadcast_in_dim.2.lv
  6.1 1.3 %pad_maximum_fusion.norms = f32[2,2,256]{2,1,0:T(2,128)} fusion(f32[1,2,256]{2,1,0:T(2,128)} %bitcast.31, f32[1,2,256]{2,1,0:T(2,128)} %bitcast.32), kind=kLoop, calls=%fused_computation | loop fusion | flops 1024 | bytes 8192 | tf_op jit(solution)/shard_map/stack | solution.py:386
  7.4 115.9 %step.1 = (bf16[64,1280]{1,0:T(8,128)(2,1)}, bf16[256,1280]{1,0:T(8,128)(2,1)}) custom-call(bf16[16,4,16,256]{3,2,1,0:T(8,128)(2,1)} %bitcast.28, bf16[4,16,1280]{2,1,0:T(8,128)(2,1)} %bitcast.29, bf16[256,1280]{1,0:T(8,128)(2,1)} %gow.1, bf16[256,1280]{1,0:T(8,128)(2,1)} %gtw.1, bf16[4,16,1280]{2,1,0:T(8,128)(2,1)} %bitcast.30, bf16[8,256]{1,0:T(8,128)(2,1)} %stack.8.emb, ...), custom_call_target="tpu_custom_call" | custom-call | tf_op jit(solution)/shard_map/step/pallas_call | solution.py:418
  123.3 1.6 %copy.18 = bf16[64,1280]{1,0:T(8,128)(2,1)} copy(bf16[64,1280]{1,0:T(8,128)(2,1)} %get-tuple-element.13) | data formatting | bytes 327680
  124.9 2.0 %copy.19 = bf16[256,1280]{1,0:T(8,128)(2,1)} copy(bf16[256,1280]{1,0:T(8,128)(2,1)} %get-tuple-element.14) | data formatting | bytes 1310720
  (4 shorter events, 0.0 us)

commit v3 on v2

--- a/solution.py
+++ b/solution.py
@@ -13,14 +13,15 @@
 F32 = jnp.float32
 MESH = pl.DeviceIdType.MESH
 FAR_FIRST = (4, 3, 5, 2, 6, 1, 7)
-
-
-def time_embed(step_value, width):
-    half_width = width // 2
-    positions = jnp.arange(half_width, dtype=F32)
-    frequencies = jnp.exp(positions * (-math.log(10000.0) / half_width))
-    angles = step_value.astype(F32) * frequencies
-    return jnp.concatenate([jnp.cos(angles), jnp.sin(angles)]).astype(BF16)
+NEAR_FIRST = (1, 7, 2, 6, 3, 5, 4)
+
+
+def time_embeds(steps):
+    row = lax.broadcasted_iota(jnp.int32, (8, 128), 0)
+    values = jnp.where(row == 0, steps[0], jnp.where(row == 1, steps[1], steps[2])).astype(F32)
+    positions = lax.broadcasted_iota(jnp.int32, (8, 128), 1).astype(F32)
+    angles = values * jnp.exp(positions * (-math.log(10000.0) / 128))
+    return jnp.concatenate([jnp.cos(angles), jnp.sin(angles)], axis=1).astype(BF16), values
 
 
 def dot(a, b):
@@ -36,7 +37,7 @@
 
 
 def kernel(
-    gh4, resid4, gow, gtw, noise4, emb, lv, tq, cq, tow, cow, ttw, ctw, norms,
+    gh4, resid4, gow, gtw, noise4, steps, tq, cq, tow, cow, ttw, ctw, t_norm, c_norm,
     latent_out, grad_out,
     heads_r, heads, ow_gen, tw_gen, resid, wq, ow, tw, nrm, gg, md,
     p1b, p1f, x1r, z1s, z1r, la, na, lat4,
@@ -115,9 +116,10 @@
     p1b[...] = part.astype(BF16).reshape(8, 16, 1280)
     pl.semaphore_wait(barrier, len(peers))
 
-    for dz in FAR_FIRST:
+    for dz in NEAR_FIRST:
         send(na.at[s], na.at[s], n_zs.at[dz], n_zr.at[z], z_dev(dz))
-    send(norms, nrm, m_s, m_r, x_dev)
+    for i, norm in enumerate((t_norm, c_norm)):
+        send(norm, nrm.at[i], m_s.at[i], m_r.at[i], x_dev)
 
     def sum_start(pb, xr_buf, xs_sem, xr_sem):
         for dz in FAR_FIRST + (0,):
@@ -134,7 +136,7 @@
     def sum_end(pf, xr_buf, xr_sem, zr_buf, zr_sem):
         got(xr_buf.at[z], xr_sem.at[z])
         total = pf[z] + xr_buf[z].astype(F32)
-        for dz in reversed(FAR_FIRST):
+        for dz in NEAR_FIRST:
             zz = z_of(dz)
             got(zr_buf.at[zz], zr_sem.at[zz])
             total = total + zr_buf[zz].astype(F32)
@@ -144,18 +146,20 @@
     p1f[...] = dot(heads_r[pl.ds(xl * 8, 8)].reshape(128, 256), ow_gen[...]).reshape(8, 16, 1280)
     sum_middle(p1f, x1r, a_xr, z1s, z1r, a_zs, a_zr)
     send(na.at[s], na.at[s], n_xs.at[z], n_xr.at[z], x_dev)
-    for dz in reversed(FAR_FIRST):
+    for dz in NEAR_FIRST:
         zz = z_of(dz)
         got(na.at[xl * 8 + zz], n_zr.at[zz])
         send(na.at[xl * 8 + zz], na.at[xl * 8 + zz], n_xs.at[zz], n_xr.at[zz], x_dev)
 
+    emb, values = time_embeds(steps)
+    noise_levels = values / 1000.0
     l_gtw.wait()
-    gg[...] = dot(emb[...], tw_gen[...])
+    gg[...] = dot(emb, tw_gen[...])
     l_tt.wait()
     l_ct.wait()
 
     def modulate(i, carry):
-        md[i // 3, lax.rem(i, 3)] = dot(emb[...], tw[i // 3, lax.rem(i, 3)])
+        md[i // 3, lax.rem(i, 3)] = dot(emb, tw[i // 3, lax.rem(i, 3)])
         return carry
 
     lax.fori_loop(0, 6, modulate, 0)
@@ -166,7 +170,7 @@
     la[s] = latent
     lat4[r] = latent
 
-    for dz in FAR_FIRST:
+    for dz in NEAR_FIRST:
         send(la.at[s], la.at[s], l_zs.at[dz], l_zr.at[z], z_dev(dz))
     send(la.at[s], la.at[s], l_xs.at[z], l_xr.at[z], x_dev)
     for d in (1, 2, 3):
@@ -182,7 +186,7 @@
         lat = la[b].astype(F32)
         noi = na[b].astype(F32)
         for level in range(2):
-            sl = lv[level : level + 1, 0:1]
+            sl = noise_levels[1 + level : 2 + level, 0:1]
             noisy = ((1.0 - sl) * lat + sl * noi).astype(BF16).astype(F32)
             square = jnp.sum(noisy * noisy, axis=1, keepdims=True)
             sqc[level, rows, :] = jnp.broadcast_to(square, (16, 128))
@@ -191,13 +195,13 @@
                 sc[level, model, rows, :] = (noisy * scale).astype(BF16)
 
     prepare(s)
-    for dz in reversed(FAR_FIRST):
+    for dz in NEAR_FIRST:
         zz = z_of(dz)
         b = xl * 8 + zz
         got(la.at[b], l_zr.at[zz])
         send(la.at[b], la.at[b], l_xs.at[zz], l_xr.at[zz], x_dev)
         prepare(b)
-    for dz in (0,) + tuple(reversed(FAR_FIRST)):
+    for dz in (0,) + NEAR_FIRST:
         zz = z_of(dz)
         b = ol * 8 + zz
         got(la.at[b], l_xr.at[zz])
@@ -240,7 +244,8 @@
         got(xqr.at[i], q_r.at[1 + i])
     square = jnp.broadcast_to((xqr[0] + xqr[1])[0:1, :], (128, 256))
     rinv = lax.rsqrt(jnp.transpose(square) * (1.0 / D) + 1e-06)
-    got(nrm, m_r)
+    for i in range(2):
+        got(nrm.at[i], m_r.at[i])
 
     def mixed_head(k, h):
         cols = slice(h * 128, h * 128 + 128)
@@ -323,10 +328,10 @@
     ga[s, r] = grad[:, pl.ds(column_start(r), 384)]
     for d in (1, 3, 2):
         got(ga.at[s, y_of(d)], g_yr.at[y_of(d)])
-    for dz in FAR_FIRST:
+    for dz in NEAR_FIRST:
         send(ga.at[s], ga.at[s], g_zs.at[dz], g_zr.at[z], z_dev(dz))
     send(ga.at[s], ga.at[s], g_xs.at[z], g_xr.at[z], x_dev)
-    for dz in reversed(FAR_FIRST):
+    for dz in NEAR_FIRST:
         zz = z_of(dz)
         b = xl * 8 + zz
         got(ga.at[b], g_zr.at[zz])
@@ -379,11 +384,6 @@
     critic_time,
     critic_norm,
 ):
-    embeds = jnp.stack([time_embed(steps[min(i, 2)], gen_time_w.shape[0]) for i in range(8)])
-    levels = jnp.broadcast_to(
-        jnp.pad(steps[1:3].astype(F32) / 1000.0, (0, 6))[:, None], (8, 128)
-    )
-    norms = jnp.stack([teacher_norm, critic_norm])
     vmem = pl.BlockSpec(memory_space=pltpu.VMEM)
     hbm = pl.BlockSpec(memory_space=pl.ANY)
     V = pltpu.VMEM
@@ -412,7 +412,7 @@
         S((8,)), S((8,)), S((8,)), S((8,)), S((4,)), S((4,)),
         S((8,)), S((8,)), S((8,)), S((8,)),
         S((4,)), S((4,)), S((8,)), S((8,)), S((8,)), S((8,)),
-        S(()), S(()), S((3,)), S((3,)), S((3, 2)), S((3, 2)), S((3, 2)), S((3, 2)),
+        S((2,)), S((2,)), S((3,)), S((3,)), S((3, 2)), S((3, 2)), S((3, 2)), S((3, 2)),
         S((2, 4)), S((2, 4)), S((4,)), S((2, 2)), S((2, 4)), S((2, 4)),
     ]
     latent, weight_grad = pl.pallas_call(
@@ -421,7 +421,7 @@
             jax.ShapeDtypeStruct((64, 1280), BF16),
             jax.ShapeDtypeStruct((256, 1280), BF16),
         ),
-        in_specs=[hbm] * 5 + [vmem] * 2 + [hbm] * 6 + [vmem],
+        in_specs=[hbm] * 5 + [pl.BlockSpec(memory_space=pltpu.SMEM)] + [hbm] * 6 + [vmem] * 2,
         out_specs=(vmem, vmem),
         scratch_shapes=scratch,
         compiler_params=pltpu.CompilerParams(
@@ -434,15 +434,15 @@
         gen_out_w,
         gen_time_w,
         noise.reshape(4, 16, 1280),
-        embeds,
-        levels,
+        steps,
         teacher_qkv.transpose(1, 0, 2),
         critic_qkv.transpose(1, 0, 2),
         teacher_out,
         critic_out,
         teacher_time.transpose(1, 0, 2),
         critic_time.transpose(1, 0, 2),
-        norms,
+        teacher_norm,
+        critic_norm,
     )
     return (latent, weight_grad)
 

time: 128 us -> 112 us (0.88)
  Pallas kernels: 116 us -> 106 us
  local copies, waits for them, and re-layouts: 6.2 us -> 3.56 us
  other arithmetic: 2.2 us -> 0 us
  between operations: 2.54 us -> 0.64 us
    pallas_call x1, Pallas kernels: 116 us -> 106 us  [on_device(): pl.pallas_call(kernel, out_shape=(jax.ShapeDtypeStruct((64, 1280), BF16),...]
    slice x1 -> x0, local copies, waits for them, and re-layouts: 1.36 us -> none  [on_device(): steps[min(i, 2)]]
    another operation x1 -> x0, other arithmetic: 1.29 us -> none  [on_device(): norms = jnp.stack([teacher_norm, critic_norm])]
where the time goes in v3:
time: 112 us; the launch traced here: 111 us
  Pallas kernels  106 us (95%)
  local copies, waits for them, and re-layouts  3.56 us (3%)
    pallas_call x1, Pallas kernels, on_device(): pl.pallas_call(kernel, out_shape=(jax.ShapeDtypeStruct((64, 1280), BF16),...  106 us
    unnamed x2, local copies, waits for them, and re-layouts  3.56 us

profile of v3, /device:TPU:2, one launch (start us, length us, event | category | flops | bytes accessed | tf_op | source)
XLA Modules:
  0.0 110.6 jit_solution(6469940003237611040)
XLA Ops:
  0.6 106.4 %step.1 = (bf16[64,1280]{1,0:T(8,128)(2,1)}, bf16[256,1280]{1,0:T(8,128)(2,1)}) custom-call(bf16[16,4,16,256]{3,2,1,0:T(8,128)(2,1)} %bitcast.11, bf16[4,16,1280]{2,1,0:T(8,128)(2,1)} %bitcast.12, bf16[256,1280]{1,0:T(8,128)(2,1)} %gow.1, bf16[256,1280]{1,0:T(8,128)(2,1)} %gtw.1, bf16[4,16,1280]{2,1,0:T(8,128)(2,1)} %bitcast.13, s32[3]{0:T(128)} %steps.1, ...), custom_call_target="tpu_custom_call" | custom-call | tf_op jit(solution)/shard_map/step/pallas_call | solution.py:418
  107.1 1.6 %copy.18 = bf16[64,1280]{1,0:T(8,128)(2,1)} copy(bf16[64,1280]{1,0:T(8,128)(2,1)} %get-tuple-element.4) | data formatting | bytes 327680
  108.7 2.0 %copy.19 = bf16[256,1280]{1,0:T(8,128)(2,1)} copy(bf16[256,1280]{1,0:T(8,128)(2,1)} %get-tuple-element.5) | data formatting | bytes 1310720

commit v4 on v3

v4 whole, which is shorter than its diff:
```python
import math

import jax
import jax.numpy as jnp
from jax import lax
from jax.experimental import pallas as pl
from jax.experimental.pallas import tpu as pltpu
from jax.sharding import PartitionSpec as P

D = 5120
HEAD_DIM = 128
BF16 = jnp.bfloat16
F32 = jnp.float32
MESH = pl.DeviceIdType.MESH
FAR_FIRST = (4, 3, 5, 2, 6, 1, 7)
NEAR_FIRST = (1, 7, 2, 6, 3, 5, 4)


def time_embeds(steps):
    row = lax.broadcasted_iota(jnp.int32, (8, 128), 0)
    values = jnp.where(row == 0, steps[0], jnp.where(row == 1, steps[1], steps[2])).astype(F32)
    positions = lax.broadcasted_iota(jnp.int32, (8, 128), 1).astype(F32)
    angles = values * jnp.exp(positions * (-math.log(10000.0) / 128))
    return jnp.concatenate([jnp.cos(angles), jnp.sin(angles)], axis=1).astype(BF16), values


def dot(a, b):
    return jnp.dot(a, b, preferred_element_type=F32)


def dot_t(a, b):
    return lax.dot_general(a, b, (((1,), (1,)), ((), ())), preferred_element_type=F32)


FRONT = ((0, 768), (768, 512))
NOISE_AT = 0
KVD = False
QO = 1
DIRECT15 = False
TAIL = ((0, 3, 6, 8), (1, 4, 7, 9), (2, 5))


def cols(i, n=1):
    return slice(i * 128, (i + n) * 128)


def kernel(
    gh4, resid4, gow, gtw, noise4, steps, tq, cq, tow, cow, ttw, ctw, t_norm, c_norm,
    latent_out, grad_out,
    heads_r, heads, ow_gen, tw_gen, resid, wq, ow, tw, nrm, gg, md,
    na, lat4, sc, sqc, sqs, cqr, sqx, xqr,
    cs, cr, of, pre, xs, xr, kvb, qb, hos, ha, acc,
    front, tail,
    lsem, n_zs, n_zr, n_xs, n_xr, l_ys, l_yr,
    m_s, m_r, q_s, q_r, c_s, c_r, x_s, x_r, kv_s, kv_r, h_s, h_r,
):
    r = lax.axis_index("role")
    s = lax.axis_index("seq")
    m = lax.axis_index("mp")
    xl, z = s // 8, lax.rem(s, 8)
    xh, c = m // 2, lax.rem(m, 2)
    ol = 1 - xl
    oc = 1 - c
    z_of = lambda dz: lax.rem(z + dz, 8)
    z_dev = lambda dz: {"seq": xl * 8 + z_of(dz)}
    x_dev = {"seq": ol * 8 + z}
    core_dev = {"mp": 2 * xh + oc}
    side_dev = lambda level: {"seq": ol * 8 + z, "mp": 2 * level + c}
    y_of = lambda d: lax.rem(r + d, 4)
    y_dev = lambda d: {"role": y_of(d)}
    below, above, across = y_of(3), y_of(1), y_of(2)
    pair, odd = r // 2, lax.rem(r, 2)
    pair_dev = {"role": 2 * pair + 1 - odd}

    def rc(src, dst, ssem, rsem, dev):
        return pltpu.make_async_remote_copy(
            src_ref=src, dst_ref=dst, send_sem=ssem, recv_sem=rsem,
            device_id=dev, device_id_type=MESH,
        )

    sent = []

    def send(*args):
        copy = rc(*args)
        copy.start()
        sent.append(copy)

    def got(dst, rsem):
        rc(dst, dst, rsem, rsem, x_dev).wait_recv()

    loads = []

    def load(src, dst):
        copy = pltpu.make_async_copy(src, dst, lsem.at[len(loads)])
        copy.start()
        loads.append(copy)
        return copy

    barrier = pltpu.get_barrier_semaphore()
    peers = [z_dev(dz) for dz in range(1, 8)] + [x_dev, core_dev]
    peers += [side_dev(1 - xh)] + [y_dev(d) for d in (1, 2, 3)]
    for dev in peers:
        pl.semaphore_signal(barrier, inc=1, device_id=dev, device_id_type=MESH)
    l_heads = load(gh4.at[:, r], heads_r)
    l_gow = load(gow, ow_gen)
    l_noise = load(noise4.at[r], na.at[s])
    l_resid = load(resid4.at[r], resid)
    l_gtw = load(gtw, tw_gen)
    l_tt = load(ttw, tw.at[0])
    l_ct = load(ctw, tw.at[1])
    l_tq = load(tq, wq.at[0])
    l_cq = load(cq, wq.at[1])
    l_to = load(tow, ow.at[0])
    l_co = load(cow, ow.at[1])
    l_all = load(gh4, heads)
    l_heads.wait()
    l_gow.wait()
    l_noise.wait()
    part = dot(heads_r[pl.ds(ol * 8, 8)].reshape(128, 256), ow_gen[...])
    for f, (start, width) in zip(front, FRONT):
        f["pb"][...] = part[:, start : start + width].astype(BF16).reshape(8, 16, width)
    pl.semaphore_wait(barrier, len(peers))

    def sum_start(f):
        for dz in FAR_FIRST + (0,):
            zz = z_of(dz)
            send(f["pb"].at[zz], f["xr"].at[zz], f["xs_s"].at[zz], f["xs_r"].at[zz], x_dev)

    def sum_middle(f):
        for dz in FAR_FIRST:
            zz = z_of(dz)
            got(f["xr"].at[zz], f["xs_r"].at[zz])
            f["zs"][zz] = (f["pf"][zz] + f["xr"][zz].astype(F32)).astype(BF16)
            send(f["zs"].at[zz], f["zr"].at[z], f["zs_s"].at[dz], f["zs_r"].at[z], z_dev(dz))

    def sum_end(f):
        got(f["xr"].at[z], f["xs_r"].at[z])
        total = f["pf"][z] + f["xr"][z].astype(F32)
        for dz in NEAR_FIRST:
            zz = z_of(dz)
            got(f["zr"].at[zz], f["zs_r"].at[zz])
            total = total + f["zr"][zz].astype(F32)
        return total

    def gather_start(f):
        own = f["ga"].at[s]
        for dz in NEAR_FIRST:
            send(own, own, f["gz_s"].at[dz], f["gz_r"].at[z], z_dev(dz))
        send(own, own, f["gx_s"].at[z], f["gx_r"].at[z], x_dev)

    def gather_step(f, dz):
        zz = z_of(dz)
        block = f["ga"].at[xl * 8 + zz]
        got(block, f["gz_r"].at[zz])
        send(block, block, f["gx_s"].at[zz], f["gx_r"].at[zz], x_dev)
        return xl * 8 + zz

    def gather_end(f, dz):
        zz = z_of(dz)
        got(f["ga"].at[ol * 8 + zz], f["gx_r"].at[zz])
        return ol * 8 + zz

    def noise_start():
        for dz in NEAR_FIRST:
            send(na.at[s], na.at[s], n_zs.at[dz], n_zr.at[z], z_dev(dz))

    if NOISE_AT == 0:
        noise_start()
    for f in front:
        sum_start(f)
    for i, norm in enumerate((t_norm, c_norm)):
        send(norm, nrm.at[i], m_s.at[i], m_r.at[i], x_dev)
    if NOISE_AT == 1:
        noise_start()
    send(na.at[s], na.at[s], n_xs.at[z], n_xr.at[z], x_dev)
    part = dot(heads_r[pl.ds(xl * 8, 8)].reshape(128, 256), ow_gen[...])
    for f, (start, width) in zip(front, FRONT):
        f["pf"][...] = part[:, start : start + width].reshape(8, 16, width)
    for n, f in enumerate(front):
        sum_middle(f)
        if n == 0 and NOISE_AT == 2:
            noise_start()
    if NOISE_AT == 3:
        noise_start()

    emb, values = time_embeds(steps)
    noise_levels = values / 1000.0
    l_gtw.wait()
    gg[...] = dot(emb, tw_gen[...])
    l_tt.wait()
    l_ct.wait()

    def modulate(i, carry):
        md[i // 3, lax.rem(i, 3)] = dot(emb, tw[i // 3, lax.rem(i, 3)])
        return carry

    lax.fori_loop(0, 6, modulate, 0)
    l_resid.wait()

    def noise_forward():
        for dz in NEAR_FIRST:
            zz = z_of(dz)
            got(na.at[xl * 8 + zz], n_zr.at[zz])
            send(na.at[xl * 8 + zz], na.at[xl * 8 + zz], n_xs.at[zz], n_xr.at[zz], x_dev)

    if NOISE_AT < 2:
        noise_forward()

    for f, (start, width) in zip(front, FRONT):
        at = slice(start, start + width)
        latent = (resid[:, at].astype(F32) + gg[0:1, at] * sum_end(f)).astype(BF16)
        f["ga"][s] = latent
        lat4[r, :, at] = latent
        gather_start(f)
    if NOISE_AT >= 2:
        noise_forward()
    for d in (1, 2, 3):
        send(lat4.at[r], lat4.at[r], l_ys.at[d], l_yr.at[r], y_dev(d))
    for level in range(2):
        for model in range(2):
            first = lax.broadcasted_iota(jnp.int32, (16, 1280), 0) == 0
            shift = md[model, 0, 1 + level : 2 + level, :]
            sc[level, model, 256:272, :] = jnp.where(first, shift, 0.0).astype(BF16)

    def prepare(f, start, width, b):
        at = slice(start, start + width)
        rows = pl.ds(pl.multiple_of(b * 16, 16), 16)
        lat = f["ga"][b].astype(F32)
        noi = na[b, :, at].astype(F32)
        for level in range(2):
            sl = noise_levels[1 + level : 2 + level, 0:1]
            noisy = ((1.0 - sl) * lat + sl * noi).astype(BF16).astype(F32)
            square = jnp.sum(noisy * noisy, axis=1, keepdims=True)
            square = jnp.broadcast_to(square, (16, 128))
            if start == 0:
                sqc[level, rows, :] = square
            else:
                sqc[level, rows, :] += square
            for model in range(2):
                scale = 1.0 + md[model, 1, 1 + level : 2 + level, at]
                sc[level, model, rows, at] = (noisy * scale).astype(BF16)

    for f, (start, width) in zip(front, FRONT):
        prepare(f, start, width, s)
        for dz in NEAR_FIRST:
            prepare(f, start, width, gather_step(f, dz))
    for dz in range(8):
        got(na.at[ol * 8 + z_of(dz)], n_xr.at[z_of(dz)])
    l_tq.wait()
    l_cq.wait()

    def product_part(level, model, kind, n):
        at = slice(FRONT[n][0], sum(FRONT[n]))
        return dot(sc[level, model, :, at], wq[model, kind, at])

    for n, (f, (start, width)) in enumerate(zip(front, FRONT)):
        for dz in (0,) + NEAR_FIRST:
            prepare(f, start, width, gather_end(f, dz))
        if n == 0:
            for level in range(2):
                pre[level] = product_part(level, oc, 1, 0)
                of[0, level] = product_part(level, c, 1, 0)

    def qkv_dots(k):
        kind = (k + 1) % 3
        for level in range(2):
            if k == 0:
                cs[k, level] = (pre[level] + product_part(level, oc, 1, 1)).astype(BF16)
            else:
                cs[k, level] = dot(sc[level, oc], wq[oc, kind]).astype(BF16)
            send(cs.at[k, level], cr.at[k, level], c_s.at[k, level], c_r.at[k, level], core_dev)
        for level in range(2):
            if k == 0:
                of[k, level] += product_part(level, c, 1, 1)
            else:
                of[k % 2, level] = dot(sc[level, c], wq[c, kind])

    def qkv_sums(k):
        for level in range(2):
            got(cr.at[k, level], c_r.at[k, level])
            xs[k, level] = (of[k % 2, level] + cr[k, level].astype(F32)).astype(BF16)
            send(xs.at[k, level], xr.at[k, xh], x_s.at[k, level], x_r.at[k, xh], side_dev(level))

    def square_send():
        for level in range(2):
            sqs[level] = jnp.transpose(sqc[level])[0:8, :]
        send(sqs, cqr, q_s.at[0], q_r.at[0], core_dev)

    def square_pass():
        got(cqr, q_r.at[0])
        sqx[...] = sqs[...] + cqr[...]
        for level in range(2):
            send(sqx.at[level], xqr.at[xh], q_s.at[1 + level], q_r.at[1 + xh], side_dev(level))

    if QO == 0:
        square_send()
        qkv_dots(0)
        square_pass()
        qkv_dots(1)
        qkv_sums(0)
        qkv_dots(2)
        qkv_sums(1)
        qkv_sums(2)
    else:
        qkv_dots(0)
        square_send()
        qkv_sums(0)
        qkv_dots(1)
        square_pass()
        qkv_sums(1)
        qkv_dots(2)
        qkv_sums(2)

    for i in range(2):
        got(xqr.at[i], q_r.at[1 + i])
    square = jnp.broadcast_to((xqr[0] + xqr[1])[0:1, :], (128, 256))
    rinv = lax.rsqrt(jnp.transpose(square) * (1.0 / D) + 1e-06)
    for i in range(2):
        got(nrm.at[i], m_r.at[i])

    def mixed_head(k, h):
        both = xr[k, 0, :, cols(h)].astype(F32) + xr[k, 1, :, cols(h)].astype(F32)
        return both[0:256] * rinv + both[256:257]

    def normed(values, gains):
        factor = lax.rsqrt(jnp.mean(values * values, axis=-1, keepdims=True) + 1e-06)
        return (values * factor * gains).astype(BF16)

    for k in range(2):
        for i in range(2):
            got(xr.at[k, i], x_r.at[k, i])
        for h in range(2):
            values = mixed_head(k, h)
            if k == 0:
                values = normed(values, nrm[c, 1:2, cols(h)])
            kvb[k, r, :, cols(h)] = values.astype(BF16)
        for d in (1, 3, 2) if KVD else (1, 3):
            send(kvb.at[k, r], kvb.at[k, r], kv_s.at[k, d], kv_r.at[k, r], y_dev(d))
    got(kvb.at[0, below], kv_r.at[0, below])
    if not KVD:
        send(kvb.at[0, below], kvb.at[0, below], kv_s.at[0, 2], kv_r.at[0, below], y_dev(1))
    for i in range(2):
        got(xr.at[2, i], x_r.at[2, i])
    for h in range(2):
        qb[h] = normed(mixed_head(2, h), nrm[c, 0:1, cols(h)])
    got(kvb.at[1, above], kv_r.at[1, above])
    if not KVD:
        send(kvb.at[1, above], kvb.at[1, above], kv_s.at[1, 2], kv_r.at[1, above], y_dev(3))
    got(kvb.at[0, above], kv_r.at[0, above])

    exponent = math.log2(math.e) / math.sqrt(HEAD_DIM)
    sums = [jnp.zeros((256, 1), F32)] * 2
    outs = [jnp.zeros((256, 128), F32)] * 2
    for n, b in enumerate((r, above, below, across)):
        if n == 2:
            got(kvb.at[1, below], kv_r.at[1, below])
        if n == 3:
            got(kvb.at[0, across], kv_r.at[0, across])
            got(kvb.at[1, across], kv_r.at[1, across])
        for h in range(2):
            e = jnp.exp2(dot_t(qb[h], kvb[0, b, :, cols(h)]) * exponent)
            sums[h] = sums[h] + jnp.sum(e, axis=1, keepdims=True)
            outs[h] = outs[h] + dot(e.astype(BF16), kvb[1, b, :, cols(h)])
            if n == 3:
                hos[h] = (outs[h] / sums[h]).astype(BF16)
                for level in range(2):
                    send(hos.at[h], ha.at[xh, c, h], h_s.at[level, h], h_r.at[xh, c, h], side_dev(level))

    l_to.wait()
    l_co.wait()

    def out_term(level, model, half):
        rows = pl.ds(pl.multiple_of(half * 128, 128), 128)
        both = jnp.concatenate([ha[level, model, h, rows] for h in range(2)], axis=1)
        sign = (model.astype(F32) - 0.5) * md[model, 2, 1 + level : 2 + level, :]
        return sign * dot(both, ow[model])

    for h in range(2):
        for level in range(2):
            block = ha.at[level, c, h]
            got(block, h_r.at[level, c, h])
            send(block, block, h_s.at[2 + level, h], h_r.at[level, c, h], core_dev)
    for half in range(2):
        acc[half] = out_term(0, c, half) + out_term(1, c, half)
    for h in range(2):
        for level in range(2):
            got(ha.at[level, oc, h], h_r.at[level, oc, h])

    def by_chunk(part, name):
        for f, tiles in zip(tail, TAIL):
            for i, tile in enumerate(tiles):
                piece = part[:, cols(tile)].reshape(8, 16, 128)
                f[name][:, :, cols(i)] = piece.astype(f[name].dtype)

    by_chunk(acc[ol] + out_term(0, oc, ol) + out_term(1, oc, ol), "pb")
    for f in tail:
        sum_start(f)
    by_chunk(acc[xl] + out_term(0, oc, xl) + out_term(1, oc, xl), "pf")
    for f in tail:
        sum_middle(f)
    for d in (1, 2, 3):
        got(lat4.at[y_of(d)], l_yr.at[y_of(d)])
    latent_out[...] = lat4[...].reshape(64, 1280)

    def finish(n):
        f, tiles = tail[n], TAIL[n]
        total = sum_end(f)
        for i, tile in enumerate(tiles):
            f["grad"][i] = (gg[0:1, cols(tile)] * total[:, cols(i)]).astype(BF16)
        if n < 2:
            for d in (2, 1, 3):
                send(f["grad"].at[y_of(d)], f["ga"].at[s, r], f["y_s"].at[d], f["y_r"].at[r], y_dev(d))
            f["ga"][s, r] = f["grad"][r]
        else:
            send(f["grad"].at[1 - odd], f["ga"].at[s, odd], f["y_s"].at[0], f["y_r"].at[odd], pair_dev)
            f["ga"][s, odd] = f["grad"][odd]

    def collect(n):
        f = tail[n]
        if n < 2:
            for d in (1, 3, 2):
                got(f["ga"].at[s, y_of(d)], f["y_r"].at[y_of(d)])
        else:
            got(f["ga"].at[s, 1 - odd], f["y_r"].at[1 - odd])
        gather_start(f)

    def grad_term(n, half):
        at = pl.ds(half * 8, 8)
        lhs = heads[at] if n < 2 else heads[at, pl.ds(2 * pair, 2)]
        rows = 512 if n < 2 else 256
        return lax.dot_general(
            lhs.reshape(rows, 256), tail[n]["ga"][at].reshape(rows, 128),
            (((0,), (0,)), ((), ())), preferred_element_type=F32,
        )

    def product(n):
        f = tail[n]
        half = grad_term(n, xl)
        for dz in range(8):
            gather_end(f, dz)
        f["wg"][r] = (half + grad_term(n, ol)).astype(BF16)
        for d in (2, 1, 3):
            send(f["wg"].at[r], f["wg"].at[r], f["w_s"].at[d], f["w_r"].at[r], y_dev(d))

    def arrived(n):
        f = tail[n]
        for b in (below, above, across):
            got(f["wg"].at[b], f["w_r"].at[b])

    finish(0)
    collect(0)
    finish(1)
    for dz in NEAR_FIRST[:3]:
        gather_step(tail[0], dz)
    collect(1)
    finish(2)
    for dz in NEAR_FIRST[3:]:
        gather_step(tail[0], dz)
    collect(2)
    l_all.wait()
    for dz in NEAR_FIRST:
        gather_step(tail[1], dz)
    product(0)
    for dz in NEAR_FIRST:
        gather_step(tail[2], dz)
    product(1)
    product(2)
    arrived(0)
    arrived(1)
    for n in range(2):
        for i, tile in enumerate(TAIL[n]):
            grad_out[:, cols(tile)] = tail[n]["wg"][i]
    arrived(2)
    for i, tile in enumerate(TAIL[2]):
        both = tail[2]["wg"][i].astype(F32) + tail[2]["wg"][i + 2].astype(F32)
        grad_out[:, cols(tile)] = both.astype(BF16)
    for copy in sent:
        copy.wait_send()


def hand_over(latent, weight_grad, latent_out, grad_out):
    latent_out[...] = latent[...]
    grad_out[...] = weight_grad[...]


def on_device(
    gen_heads,
    gen_resid,
    gen_out_w,
    gen_time_w,
    noise,
    steps,
    teacher_qkv,
    teacher_out,
    teacher_time,
    teacher_norm,
    critic_qkv,
    critic_out,
    critic_time,
    critic_norm,
):
    vmem = pl.BlockSpec(memory_space=pltpu.VMEM)
    hbm = pl.BlockSpec(memory_space=pl.ANY)
    V = pltpu.VMEM
    S = pltpu.SemaphoreType.DMA
    block = (16, 1280)
    sums = lambda width: {
        "pb": V((8, 16, width), BF16), "pf": V((8, 16, width), F32),
        "xr": V((8, 16, width), BF16), "zs": V((8, 16, width), BF16), "zr": V((8, 16, width), BF16),
        "xs_s": S((8,)), "xs_r": S((8,)), "zs_s": S((8,)), "zs_r": S((8,)),
        "gz_s": S((8,)), "gz_r": S((8,)), "gx_s": S((8,)), "gx_r": S((8,)),
    }
    front = [{**sums(width), "ga": V((16, 16, width), BF16)} for _, width in FRONT]
    tail = [
        {
            **sums(128 * len(tiles)),
            "grad": V((len(tiles), 16, 128), BF16),
            "ga": V((16, len(tiles), 16, 128), BF16),
            "wg": V((4, 256, 128), BF16),
            "y_s": S((4,)), "y_r": S((4,)), "w_s": S((4,)), "w_r": S((4,)),
        }
        for tiles in TAIL
    ]
    scratch = [
        V((16, 16, 256), BF16), V((16, 4, 16, 256), BF16), V((256, 1280), BF16),
        V((256, 1280), BF16), V(block, BF16), V((2, 3, 1280, 256), BF16),
        V((2, 256, 1280), BF16), V((2, 3, 256, 1280), BF16), V((2, 2, 256), F32),
        V((8, 1280), F32), V((2, 3, 8, 1280), F32),
        V((16,) + block, BF16), V((4,) + block, BF16),
        V((2, 2, 272, 1280), BF16), V((2, 256, 128), F32),
        V((2, 8, 256), F32), V((2, 8, 256), F32), V((2, 8, 256), F32), V((2, 8, 256), F32),
        V((3, 2, 272, 256), BF16), V((3, 2, 272, 256), BF16), V((2, 2, 272, 256), F32), V((2, 272, 256), F32),
        V((3, 2, 272, 256), BF16), V((3, 2, 272, 256), BF16),
        V((2, 4, 256, 256), BF16), V((2, 256, 128), BF16), V((2, 256, 128), BF16),
        V((2, 2, 2, 256, 128), BF16), V((2, 128, 1280), F32),
        front, tail,
        S((12,)), S((8,)), S((8,)), S((8,)), S((8,)), S((4,)), S((4,)),
        S((2,)), S((2,)), S((3,)), S((3,)), S((3, 2)), S((3, 2)), S((3, 2)), S((3, 2)),
        S((2, 4)), S((2, 4)), S((4, 2)), S((2, 2, 2)),
    ]
    latent, weight_grad = pl.pallas_call(
        kernel,
        out_shape=(
            jax.ShapeDtypeStruct((64, 1280), BF16),
            jax.ShapeDtypeStruct((256, 1280), BF16),
        ),
        in_specs=[hbm] * 5 + [pl.BlockSpec(memory_space=pltpu.SMEM)] + [hbm] * 6 + [vmem] * 2,
        out_specs=(vmem, vmem),
        scratch_shapes=scratch,
        compiler_params=pltpu.CompilerParams(
            collective_id=0, has_side_effects=True, vmem_limit_bytes=60 * 1024 * 1024
        ),
        name="step",
    )(
        gen_heads.reshape(16, 4, 16, 256),
        gen_resid.reshape(4, 16, 1280),
        gen_out_w,
        gen_time_w,
        noise.reshape(4, 16, 1280),
        steps,
        teacher_qkv.transpose(1, 0, 2),
        critic_qkv.transpose(1, 0, 2),
        teacher_out,
        critic_out,
        teacher_time.transpose(1, 0, 2),
        critic_time.transpose(1, 0, 2),
        teacher_norm,
        critic_norm,
    )
    return pl.pallas_call(
        hand_over,
        out_shape=(
            jax.ShapeDtypeStruct((64, 1280), BF16),
            jax.ShapeDtypeStruct((256, 1280), BF16),
        ),
        in_specs=[vmem, vmem],
        out_specs=(vmem, vmem),
        compiler_params=pltpu.CompilerParams(vmem_limit_bytes=8 * 1024 * 1024),
        name="hand_over",
    )(latent, weight_grad)


def solution(mesh):
    in_specs = (
        P(None, "seq"),
        P("seq", "mp"),
        P("seq", "mp"),
        P(None, "mp"),
        P("seq", "mp"),
        P(),
        P("mp", None, "seq"),
        P("seq", "mp"),
        P(None, None, "mp"),
        P(None, "seq"),
        P("mp", None, "seq"),
        P("seq", "mp"),
        P(None, None, "mp"),
        P(None, "seq"),
    )
    out_specs = (P("seq", "mp"), P("seq", "mp"))
    return jax.shard_map(
        on_device, mesh=mesh, in_specs=in_specs, out_specs=out_specs, check_vma=False
    )
```

time: 112 us -> 104 us (0.929); the launches traced: 111 us -> 104 us
  Pallas kernels: 106 us -> 101 us
  local copies, waits for them, and re-layouts: 3.56 us -> 2 us
    pallas_call x1, Pallas kernels: 106 us -> 100 us  [on_device(): pl.pallas_call(kernel, out_shape=(jax.ShapeDtypeStruct((64, 1280), BF16),...]
    unnamed x2 -> x4, local copies, waits for them, and re-layouts: 3.56 us -> 2 us
where the time goes in v4:
time: 104 us
  Pallas kernels  101 us (97%)
  local copies, waits for them, and re-layouts  2 us (2%)
    pallas_call x1, Pallas kernels, on_device(): pl.pallas_call(kernel, out_shape=(jax.ShapeDtypeStruct((64, 1280), BF16),...  100 us

profile of v4, /device:TPU:2, one launch (start us, length us, event | category | flops | bytes accessed | tf_op | source)
XLA Modules:
  0.0 103.8 jit_solution(8665245459485747889)
XLA Ops:
  0.6 100.2 %step.1 = (bf16[64,1280]{1,0:T(8,128)(2,1)}, bf16[256,1280]{1,0:T(8,128)(2,1)}) custom-call(bf16[16,4,16,256]{3,2,1,0:T(8,128)(2,1)} %bitcast.11, bf16[4,16,1280]{2,1,0:T(8,128)(2,1)} %bitcast.12, bf16[256,1280]{1,0:T(8,128)(2,1)} %gow.1, bf16[256,1280]{1,0:T(8,128)(2,1)} %gtw.1, bf16[4,16,1280]{2,1,0:T(8,128)(2,1)} %bitcast.13, s32[3]{0:T(128)} %steps.1, ...), custom_call_target="tpu_custom_call" | custom-call | tf_op jit(solution)/shard_map/step/pallas_call | solution.py:541
  100.8 0.0 copy-start
  100.9 1.1 %copy-done = bf16[256,1280]{1,0:T(8,128)(2,1)S(1)} copy-done((bf16[256,1280]{1,0:T(8,128)(2,1)S(1)}, bf16[256,1280]{1,0:T(8,128)(2,1)}, u32[]{:S(2)}) %copy-start) | copy-done | bytes 655384
  101.9 0.0 copy-start.1
  101.9 0.9 copy-done.1
  102.8 0.9 hand_over.1
Async XLA Ops:
  100.8 1.1 %copy-start = (bf16[256,1280]{1,0:T(8,128)(2,1)S(1)}, bf16[256,1280]{1,0:T(8,128)(2,1)}, u32[]{:S(2)}) copy-start(bf16[256,1280]{1,0:T(8,128)(2,1)} %get-tuple-element.5.weight_grad) | copy-start | bytes 1966084
  101.9 0.9 copy-start.1

commit v5 on v4

--- a/solution.py
+++ b/solution.py
@@ -33,10 +33,7 @@
 
 
 FRONT = ((0, 768), (768, 512))
-NOISE_AT = 0
-KVD = False
-QO = 1
-DIRECT15 = False
+NEAR, FAR = NEAR_FIRST[:4], NEAR_FIRST[4:]
 TAIL = ((0, 3, 6, 8), (1, 4, 7, 9), (2, 5))
 
 
@@ -160,28 +157,29 @@
         got(f["ga"].at[ol * 8 + zz], f["gx_r"].at[zz])
         return ol * 8 + zz
 
-    def noise_start():
-        for dz in NEAR_FIRST:
+    def noise_start(distances):
+        for dz in distances:
             send(na.at[s], na.at[s], n_zs.at[dz], n_zr.at[z], z_dev(dz))
 
-    if NOISE_AT == 0:
-        noise_start()
+    def noise_forward(distances):
+        for dz in distances:
+            zz = z_of(dz)
+            got(na.at[xl * 8 + zz], n_zr.at[zz])
+            send(na.at[xl * 8 + zz], na.at[xl * 8 + zz], n_xs.at[zz], n_xr.at[zz], x_dev)
+
+    noise_start(NEAR)
     for f in front:
         sum_start(f)
     for i, norm in enumerate((t_norm, c_norm)):
         send(norm, nrm.at[i], m_s.at[i], m_r.at[i], x_dev)
-    if NOISE_AT == 1:
-        noise_start()
     send(na.at[s], na.at[s], n_xs.at[z], n_xr.at[z], x_dev)
     part = dot(heads_r[pl.ds(xl * 8, 8)].reshape(128, 256), ow_gen[...])
     for f, (start, width) in zip(front, FRONT):
         f["pf"][...] = part[:, start : start + width].reshape(8, 16, width)
-    for n, f in enumerate(front):
+    for f in front:
         sum_middle(f)
-        if n == 0 and NOISE_AT == 2:
-            noise_start()
-    if NOISE_AT == 3:
-        noise_start()
+    noise_start(FAR)
+    noise_forward(NEAR)
 
     emb, values = time_embeds(steps)
     noise_levels = values / 1000.0
@@ -197,23 +195,13 @@
     lax.fori_loop(0, 6, modulate, 0)
     l_resid.wait()
 
-    def noise_forward():
-        for dz in NEAR_FIRST:
-            zz = z_of(dz)
-            got(na.at[xl * 8 + zz], n_zr.at[zz])
-            send(na.at[xl * 8 + zz], na.at[xl * 8 + zz], n_xs.at[zz], n_xr.at[zz], x_dev)
-
-    if NOISE_AT < 2:
-        noise_forward()
-
     for f, (start, width) in zip(front, FRONT):
         at = slice(start, start + width)
         latent = (resid[:, at].astype(F32) + gg[0:1, at] * sum_end(f)).astype(BF16)
         f["ga"][s] = latent
         lat4[r, :, at] = latent
         gather_start(f)
-    if NOISE_AT >= 2:
-        noise_forward()
+    noise_forward(FAR)
     for d in (1, 2, 3):
         send(lat4.at[r], lat4.at[r], l_ys.at[d], l_yr.at[r], y_dev(d))
     for level in range(2):
@@ -261,7 +249,7 @@
                 pre[level] = product_part(level, oc, 1, 0)
                 of[0, level] = product_part(level, c, 1, 0)
 
-    def qkv_dots(k):
+    def other_dots(k):
         kind = (k + 1) % 3
         for level in range(2):
             if k == 0:
@@ -269,12 +257,19 @@
             else:
                 cs[k, level] = dot(sc[level, oc], wq[oc, kind]).astype(BF16)
             send(cs.at[k, level], cr.at[k, level], c_s.at[k, level], c_r.at[k, level], core_dev)
+
+    def own_dots(k):
+        kind = (k + 1) % 3
         for level in range(2):
             if k == 0:
                 of[k, level] += product_part(level, c, 1, 1)
             else:
                 of[k % 2, level] = dot(sc[level, c], wq[c, kind])
 
+    def qkv_dots(k):
+        other_dots(k)
+        own_dots(k)
+
     def qkv_sums(k):
         for level in range(2):
             got(cr.at[k, level], c_r.at[k, level])
@@ -292,24 +287,16 @@
         for level in range(2):
             send(sqx.at[level], xqr.at[xh], q_s.at[1 + level], q_r.at[1 + xh], side_dev(level))
 
-    if QO == 0:
-        square_send()
-        qkv_dots(0)
-        square_pass()
-        qkv_dots(1)
-        qkv_sums(0)
-        qkv_dots(2)
-        qkv_sums(1)
-        qkv_sums(2)
-    else:
-        qkv_dots(0)
-        square_send()
-        qkv_sums(0)
-        qkv_dots(1)
-        square_pass()
-        qkv_sums(1)
-        qkv_dots(2)
-        qkv_sums(2)
+    qkv_dots(0)
+    square_send()
+    other_dots(1)
+    qkv_sums(0)
+    own_dots(1)
+    square_pass()
+    other_dots(2)
+    qkv_sums(1)
+    own_dots(2)
+    qkv_sums(2)
 
     for i in range(2):
         got(xqr.at[i], q_r.at[1 + i])
@@ -334,18 +321,16 @@
             if k == 0:
                 values = normed(values, nrm[c, 1:2, cols(h)])
             kvb[k, r, :, cols(h)] = values.astype(BF16)
-        for d in (1, 3, 2) if KVD else (1, 3):
+        for d in (1, 3):
             send(kvb.at[k, r], kvb.at[k, r], kv_s.at[k, d], kv_r.at[k, r], y_dev(d))
     got(kvb.at[0, below], kv_r.at[0, below])
-    if not KVD:
-        send(kvb.at[0, below], kvb.at[0, below], kv_s.at[0, 2], kv_r.at[0, below], y_dev(1))
+    send(kvb.at[0, below], kvb.at[0, below], kv_s.at[0, 2], kv_r.at[0, below], y_dev(1))
     for i in range(2):
         got(xr.at[2, i], x_r.at[2, i])
     for h in range(2):
         qb[h] = normed(mixed_head(2, h), nrm[c, 0:1, cols(h)])
     got(kvb.at[1, above], kv_r.at[1, above])
-    if not KVD:
-        send(kvb.at[1, above], kvb.at[1, above], kv_s.at[1, 2], kv_r.at[1, above], y_dev(3))
+    send(kvb.at[1, above], kvb.at[1, above], kv_s.at[1, 2], kv_r.at[1, above], y_dev(3))
     got(kvb.at[0, above], kv_r.at[0, above])
 
     exponent = math.log2(math.e) / math.sqrt(HEAD_DIM)
@@ -478,9 +463,22 @@
         copy.wait_send()
 
 
-def hand_over(latent, weight_grad, latent_out, grad_out):
-    latent_out[...] = latent[...]
-    grad_out[...] = weight_grad[...]
+def hand_over(latent, weight_grad, latent_out, grad_out, la, wg, sem):
+    pieces = [(latent, la, latent_out)]
+    for i in range(2):
+        rows = pl.ds(i * 128, 128)
+        pieces.append((weight_grad.at[rows], wg.at[rows], grad_out.at[rows]))
+    copies = [
+        (pltpu.make_async_copy(src, mid, sem.at[0, i]), pltpu.make_async_copy(mid, dst, sem.at[1, i]))
+        for i, (src, mid, dst) in enumerate(pieces)
+    ]
+    for into, _ in copies:
+        into.start()
+    for into, out in copies:
+        into.wait()
+        out.start()
+    for _, out in copies:
+        out.wait()
 
 
 def on_device(
@@ -573,9 +571,10 @@
             jax.ShapeDtypeStruct((64, 1280), BF16),
             jax.ShapeDtypeStruct((256, 1280), BF16),
         ),
-        in_specs=[vmem, vmem],
-        out_specs=(vmem, vmem),
-        compiler_params=pltpu.CompilerParams(vmem_limit_bytes=8 * 1024 * 1024),
+        in_specs=[hbm, hbm],
+        out_specs=(hbm, hbm),
+        scratch_shapes=[V((64, 1280), BF16), V((256, 1280), BF16), S((2, 3))],
+        compiler_params=pltpu.CompilerParams(vmem_limit_bytes=60 * 1024 * 1024),
         name="hand_over",
     )(latent, weight_grad)
 

time: 104 us -> 102 us (0.981)
  local copies, waits for them, and re-layouts: 2 us -> 0 us
    unnamed x4 -> x0, local copies, waits for them, and re-layouts: 2 us -> none
where the time goes in v5:
time: 102 us
  Pallas kernels  101 us (99%)
    pallas_call x1, Pallas kernels, on_device(): pl.pallas_call(kernel, out_shape=(jax.ShapeDtypeStruct((64, 1280), BF16),...  99.5 us

profile of v5, /device:TPU:2, one launch (start us, length us, event | category | flops | bytes accessed | tf_op | source)
XLA Modules:
  0.0 102.1 jit_solution(14486157844829858132)
XLA Ops:
  0.6 99.5 %step.1 = (bf16[64,1280]{1,0:T(8,128)(2,1)}, bf16[256,1280]{1,0:T(8,128)(2,1)}) custom-call(bf16[16,4,16,256]{3,2,1,0:T(8,128)(2,1)} %bitcast.11, bf16[4,16,1280]{2,1,0:T(8,128)(2,1)} %bitcast.12, bf16[256,1280]{1,0:T(8,128)(2,1)} %gow.1, bf16[256,1280]{1,0:T(8,128)(2,1)} %gtw.1, bf16[4,16,1280]{2,1,0:T(8,128)(2,1)} %bitcast.13, s32[3]{0:T(128)} %steps.1, ...), custom_call_target="tpu_custom_call" | custom-call | tf_op jit(solution)/shard_map/step/pallas_call | solution.py:539
  100.2 1.9 %hand_over.1 = (bf16[64,1280]{1,0:T(8,128)(2,1)}, bf16[256,1280]{1,0:T(8,128)(2,1)}) custom-call(bf16[64,1280]{1,0:T(8,128)(2,1)} %get-tuple-element.4.latent, bf16[256,1280]{1,0:T(8,128)(2,1)} %get-tuple-element.5.weight_grad), custom_call_target="tpu_custom_call" | custom-call | tf_op jit(solution)/shard_map/hand_over/pallas_call | solution.py:568

commit v6 on v5

--- a/solution.py
+++ b/solution.py
@@ -113,9 +113,13 @@
     l_heads.wait()
     l_gow.wait()
     l_noise.wait()
-    part = dot(heads_r[pl.ds(ol * 8, 8)].reshape(128, 256), ow_gen[...])
-    for f, (start, width) in zip(front, FRONT):
-        f["pb"][...] = part[:, start : start + width].astype(BF16).reshape(8, 16, width)
+
+    def first_part(n):
+        start, width = FRONT[n]
+        part = dot(heads_r[pl.ds(ol * 8, 8)].reshape(128, 256), ow_gen[:, start : start + width])
+        front[n]["pb"][...] = part.astype(BF16).reshape(8, 16, width)
+
+    first_part(0)
     pl.semaphore_wait(barrier, len(peers))
 
     def sum_start(f):
@@ -168,8 +172,9 @@
             send(na.at[xl * 8 + zz], na.at[xl * 8 + zz], n_xs.at[zz], n_xr.at[zz], x_dev)
 
     noise_start(NEAR)
-    for f in front:
-        sum_start(f)
+    sum_start(front[0])
+    first_part(1)
+    sum_start(front[1])
     for i, norm in enumerate((t_norm, c_norm)):
         send(norm, nrm.at[i], m_s.at[i], m_r.at[i], x_dev)
     send(na.at[s], na.at[s], n_xs.at[z], n_xr.at[z], x_dev)
@@ -371,15 +376,15 @@
         for level in range(2):
             got(ha.at[level, oc, h], h_r.at[level, oc, h])
 
-    def by_chunk(part, name):
+    def by_chunk(part, name, start=False):
         for f, tiles in zip(tail, TAIL):
             for i, tile in enumerate(tiles):
                 piece = part[:, cols(tile)].reshape(8, 16, 128)
                 f[name][:, :, cols(i)] = piece.astype(f[name].dtype)
-
-    by_chunk(acc[ol] + out_term(0, oc, ol) + out_term(1, oc, ol), "pb")
-    for f in tail:
-        sum_start(f)
+            if start:
+                sum_start(f)
+
+    by_chunk(acc[ol] + out_term(0, oc, ol) + out_term(1, oc, ol), "pb", True)
     by_chunk(acc[xl] + out_term(0, oc, xl) + out_term(1, oc, xl), "pf")
     for f in tail:
         sum_middle(f)

time: 102 us -> 102 us (level)
  no operation moved by 1% of the time
where the time goes in v6:
time: 102 us
  Pallas kernels  102 us (100%)
    pallas_call x1, Pallas kernels, on_device(): pl.pallas_call(kernel, out_shape=(jax.ShapeDtypeStruct((64, 1280), BF16),...  99.7 us

profile of v6, /device:TPU:2, one launch (start us, length us, event | category | flops | bytes accessed | tf_op | source)
XLA Modules:
  0.0 102.3 jit_solution(3914238511883552465)
XLA Ops:
  0.6 99.7 %step.1 = (bf16[64,1280]{1,0:T(8,128)(2,1)}, bf16[256,1280]{1,0:T(8,128)(2,1)}) custom-call(bf16[16,4,16,256]{3,2,1,0:T(8,128)(2,1)} %bitcast.11, bf16[4,16,1280]{2,1,0:T(8,128)(2,1)} %bitcast.12, bf16[256,1280]{1,0:T(8,128)(2,1)} %gow.1, bf16[256,1280]{1,0:T(8,128)(2,1)} %gtw.1, bf16[4,16,1280]{2,1,0:T(8,128)(2,1)} %bitcast.13, s32[3]{0:T(128)} %steps.1, ...), custom_call_target="tpu_custom_call" | custom-call | tf_op jit(solution)/shard_map/step/pallas_call | solution.py:544
  100.3 1.9 %hand_over.1 = (bf16[64,1280]{1,0:T(8,128)(2,1)}, bf16[256,1280]{1,0:T(8,128)(2,1)}) custom-call(bf16[64,1280]{1,0:T(8,128)(2,1)} %get-tuple-element.4.latent, bf16[256,1280]{1,0:T(8,128)(2,1)} %get-tuple-element.5.weight_grad), custom_call_target="tpu_custom_call" | custom-call | tf_op jit(solution)/shard_map/hand_over/pallas_call | solution.py:573
